TPU v7x, 512 devices: a whole 4x4x16 slice. The times are simulated.
512 devices in a mesh: ep: 128 (over y_lo, x, z), dp: 4 (over y_hi, core).
Axes of the slice: x: 4, y: 4 (y_hi: 2, y_lo: 2; y = y_hi * 2 + y_lo), z: 16, core: 2. Of those that a mesh axis runs over, the one named last changes fastest.
Arguments:
- tokens: bfloat16 [32768, 2048], P(('dp', 'ep')), parts along dimension 0, may hold values from -6 to 6
- gates: float32 [32768, 8], P(('dp', 'ep')), parts along dimension 0, may hold values from 0.05 to 1
- expert_ids: int32 [32768, 8], P(('dp', 'ep')), parts along dimension 0, may hold values from 0 to 31, all different within a row; in each aligned block of 64 rows (0 to 63, 64 to 127, ...) at most 20 rows name the same one
- slot_expert: int32 [128], P('dp'), parts along dimension 0, may hold values from 0 to 31, each once
- w_in: bfloat16 [512, 2, 192, 2048], P(('dp', 'ep')), parts along dimension 0, may hold values from -0.125 to 0.125
- w_out: bfloat16 [512, 192, 2048], P(('dp', 'ep')), parts along dimension 0, may hold values from -0.21875 to 0.21875
Outputs:
- mixed: bfloat16 [32768, 2048], P(('dp', 'ep')), parts along dimension 0
There are 4 independent parts, one for each index of `dp`. A program takes and returns all parts, laid end to end along the dimension named above; each array names one. Nothing has to cross between parts.
All inputs are finite; a program needn't handle non-finite values.
Results may differ from a plain program's by a relative error of at most 0.0058.
Values may be sent and summed in bfloat16 or wider, within the bound.
A program may use at most 64 MiB of HBM per device.

v0:
```python
import jax
import jax.numpy as jnp
from jax import lax
from jax.sharding import PartitionSpec as P

GROUP = 4
BLOCK = 128


def from_partner(block, axis, apart):
    count = lax.axis_size(axis)
    route = []
    for low in range(count):
        high = low | 1 << apart
        if high != low and high < count:
            route += [(low, high), (high, low)]
    return lax.ppermute(block, axis, route)


def local(tokens, gates, expert_ids, slot_expert, w_in, w_out):
    members = lax.axis_size("ep")
    myself = lax.axis_index("ep")
    tok_rows, width = tokens.shape
    top_count = expert_ids.shape[1]
    experts = members // GROUP
    cap_expert = min(tok_rows, 5 * tok_rows * top_count // (4 * experts))
    cap_member = (cap_expert + GROUP - 1) // GROUP
    slot_total = members * cap_member
    block_limit = slot_total // BLOCK + 1
    expert_range = jnp.arange(experts, dtype=jnp.int32)
    home = jnp.sum(
        jnp.where(slot_expert[:, None] == expert_range[None, :], expert_range[:, None], 0), axis=0
    )
    pieces_in, pieces_out = (w_in, w_out)
    bit_order = (0, 1)
    for swap_bit in bit_order:
        other_in, other_out = from_partner((pieces_in, pieces_out), "ep", swap_bit)
        lower = myself // (1 << swap_bit) % 2 == 0
        pieces_in = jnp.where(
            lower,
            jnp.concatenate([pieces_in, other_in], axis=0),
            jnp.concatenate([other_in, pieces_in], axis=0),
        )
        pieces_out = jnp.where(
            lower,
            jnp.concatenate([pieces_out, other_out], axis=0),
            jnp.concatenate([other_out, pieces_out], axis=0),
        )
    flat_ids = expert_ids.reshape(-1)
    onehot = (flat_ids[:, None] == expert_range[None, :]).astype(jnp.int32)
    rank = jnp.sum(jnp.cumsum(onehot, axis=0) * onehot, axis=1) - 1
    group = jnp.sum(onehot * home[None, :], axis=1)
    member = rank // cap_member
    slot = rank % cap_member
    slot_index = (group * GROUP + member) * cap_member + slot
    repeated = jnp.repeat(tokens, top_count, axis=0)
    send_rows = jnp.zeros((slot_total, width), jnp.bfloat16).at[slot_index].set(repeated)
    send_flag = (
        jnp.zeros((slot_total,), jnp.bfloat16).at[slot_index].set(jnp.ones((), jnp.bfloat16))
    )
    recv_rows, recv_flag = (
        lax.all_to_all(send_rows, "ep", split_axis=0, concat_axis=0, tiled=True),
        lax.all_to_all(send_flag, "ep", split_axis=0, concat_axis=0, tiled=True),
    )
    valid = recv_flag > 0.5
    valid_count = jnp.sum(valid.astype(jnp.int32))
    blocks_total = (valid_count + BLOCK - 1) // BLOCK
    position = jnp.where(valid, jnp.cumsum(valid.astype(jnp.int32)) - 1, block_limit * BLOCK)
    compact = (
        jnp.zeros((block_limit * BLOCK, width), jnp.bfloat16)
        .at[position]
        .set(recv_rows, mode="drop")
    )
    gate_weights = pieces_in[:, 0]
    up_weights = pieces_in[:, 1]

    def compute_block(block, result):
        block_rows = lax.dynamic_slice_in_dim(compact, block * BLOCK, BLOCK, 0)
        gate_part = jnp.einsum(
            "rd,jfd->rjf", block_rows, gate_weights, preferred_element_type=jnp.float32
        )
        up_part = jnp.einsum(
            "rd,jfd->rjf", block_rows, up_weights, preferred_element_type=jnp.float32
        )
        hidden = (jax.nn.silu(gate_part) * up_part).astype(jnp.bfloat16)
        produced = jnp.einsum(
            "rjf,jfd->rd", hidden, pieces_out, preferred_element_type=jnp.float32
        ).astype(jnp.bfloat16)
        return lax.dynamic_update_slice_in_dim(result, produced, block * BLOCK, 0)

    computed = lax.fori_loop(
        0, blocks_total, compute_block, jnp.zeros((block_limit * BLOCK, width), jnp.bfloat16)
    )
    back_rows = jnp.where(
        valid[:, None],
        computed[jnp.minimum(position, block_limit * BLOCK - 1)],
        jnp.zeros((), jnp.bfloat16),
    )
    returned = lax.all_to_all(back_rows, "ep", split_axis=0, concat_axis=0, tiled=True)
    gathered = returned[slot_index].reshape(tok_rows, top_count, width)
    total = jnp.zeros((tok_rows, width), jnp.float32)
    for choice_index in range(top_count):
        total = total + gates[:, choice_index][:, None] * gathered[:, choice_index].astype(
            jnp.float32
        )
    return total.astype(jnp.bfloat16)


def solution(mesh):
    return jax.shard_map(
        local,
        mesh=mesh,
        in_specs=(
            P(("dp", "ep"), None),
            P(("dp", "ep"), None),
            P(("dp", "ep"), None),
            P("dp"),
            P(("dp", "ep"), None, None, None),
            P(("dp", "ep"), None, None),
        ),
        out_specs=P(("dp", "ep"), None),
        check_vma=False,
    )
```

profile of v0, /device:TPU:66, one launch (start us, length us, event | category | flops | bytes accessed | tf_op | source)
XLA Modules:
  0.0 790.5 jit_solution(12244093465518118409)
XLA Ops:
  3.4 3.8 scatter_custom_fusion
  8.0 19.5 %all-to-all-start = ((bf16[128,5,1]{1,2,0:T(2,128)(2,1)}), bf16[128,5,1]{1,2,0:T(2,128)(2,1)S(1)}, u32[]{:S(2)}, u32[]{:S(2)}) async-start(bf16[128,5,1]{1,2,0:T(2,128)(2,1)} %all_to_all.27), calls=%async_computation | async-start | bytes 131072 | tf_op jit(solution)/shard_map/all_to_all | solution.py:63
  27.6 4.4 scatter_custom_fusion.1
  34.9 5.9 all-to-all-done
  40.8 11.9 %all-to-all-start.1 = ((bf16[128,5,2048]{2,1,0:T(8,128)(2,1)}), bf16[128,5,2048]{2,1,0:T(8,128)(2,1)}, u32[]{:S(2)}, u32[]{:S(2)}) async-start(bf16[128,5,2048]{2,1,0:T(8,128)(2,1)} %all_to_all.22), calls=%async_computation.1 | async-start | bytes 8388608 | tf_op jit(solution)/shard_map/all_to_all | solution.py:62
  52.7 3.4 collective-permute-start
  56.1 210.2 %collective-permute-done = bf16[1,2,192,2048]{3,2,0,1:T(8,128)(2,1)} collective-permute-done((bf16[1,2,192,2048]{3,2,0,1:T(8,128)(2,1)S(1)}, bf16[1,2,192,2048]{3,2,0,1:T(8,128)(2,1)}, u32[]{:S(2)}, u32[]{:S(2)}) %collective-permute-start) | collective-permute-done | bytes 1572896 | tf_op jit(solution)/shard_map/ppermute | solution.py:17
  274.5 82.5 %collective-permute-done.2 = bf16[1,192,2048]{2,1,0:T(8,128)(2,1)S(1)} collective-permute-done((bf16[1,192,2048]{2,1,0:T(8,128)(2,1)S(1)}, bf16[1,192,2048]{2,1,0:T(8,128)(2,1)S(1)}, u32[]{:S(2)}, u32[]{:S(2)}) %collective-permute-start.2) | collective-permute-done | bytes 786464 | tf_op jit(solution)/shard_map/ppermute | solution.py:17
  363.3 110.3 %collective-permute-done.3 = bf16[2,192,2048]{2,1,0:T(8,128)(2,1)} collective-permute-done((bf16[2,192,2048]{2,1,0:T(8,128)(2,1)}, bf16[2,192,2048]{2,1,0:T(8,128)(2,1)}, u32[]{:S(2)}, u32[]{:S(2)}) %collective-permute-start.3) | collective-permute-done | bytes 1572896 | tf_op jit(solution)/shard_map/ppermute | solution.py:17
  473.5 4.2 maximum_select_fusion.2
  477.7 3.9 maximum_select_fusion
  484.9 4.2 reshape.274
  489.1 8.9 %scatter_custom_fusion.2 = bf16[768,2048]{1,0:T(8,128)(2,1)} fusion(s32[640]{0:T(1024)S(1)} %get-tuple-element.45, bf16[640,2048]{1,0:T(8,128)(2,1)S(1)} %reshape.274, bf16[]{:T(256)} %constant.102.clone.1), kind=kCustom, calls=%fused_computation.33 | custom fusion | bytes 3145730 | tf_op jit(solution)/shard_map/scatter | solution.py:72
  498.3 46.0 %while.10 = (s32[]{:T(128)}, bf16[768,2048]{1,0:T(8,128)(2,1)S(1)}, s32[]{:T(128)}, bf16[768,2048]{1,0:T(8,128)(2,1)}, bf16[4,192,2048]{2,1,0:T(8,128)(2,1)}, /*...) while((s32[]{:T(128)}, bf16[768,2048]{1,0:T(8,128)(2,1)S(1)}, ...), condition=%wide.region_12.13_spmd, body=%wide.region_11.12_spmd.sunk | while | flops 1208811520 | bytes 11797663 | solution.py:91
  498.3 3.8 fusion.59
  502.1 5.3 fusion.60
  507.5 3.8 fusion.59
  511.3 5.3 fusion.60
  516.6 3.8 fusion.59
  520.4 5.3 fusion.60
  525.8 3.8 fusion.59
  529.6 5.3 fusion.60
  534.9 3.8 fusion.59
  538.7 5.3 fusion.60
  544.3 4.1 gather_fusion
  548.4 5.5 gather.9
  553.8 4.6 broadcast_select_fusion
  558.4 20.5 %all-to-all-start.2 = ((bf16[128,5,2048]{2,1,0:T(8,128)(2,1)}), bf16[128,5,2048]{2,1,0:T(8,128)(2,1)}, u32[]{:S(2)}, u32[]{:S(2)}) async-start(bf16[128,5,2048]{2,1,0:T(8,128)(2,1)} %broadcast_select_fusion), calls=%async_computation.2 | async-start | bytes 8388608 | tf_op jit(solution)/shard_map/all_to_all | solution.py:99
  579.0 189.3 %all-to-all-done.2 = bf16[128,5,2048]{2,1,0:T(8,128)(2,1)} async-done(((bf16[128,5,2048]{2,1,0:T(8,128)(2,1)}), bf16[128,5,2048]{2,1,0:T(8,128)(2,1)}, u32[]{:S(2)}, u32[]{:S(2)}) %all-to-all-start.2) | async-done | bytes 2621472 | tf_op jit(solution)/shard_map/all_to_all | solution.py:99
  768.2 4.2 all_to_all.26
  772.4 3.3 gather_fusion.1
  775.8 11.9 %fusion.43 = (bf16[64,1,2048]{2,1,0:T(2,128)(2,1)S(1)}, bf16[64,1,2048]{2,1,0:T(2,128)(2,1)S(1)}, bf16[64,1,2048]{2,1,0:T(2,128)(2,1)S(1)}, bf16[64,1,2048]{2,1,...) fusion(bf16[64,8,2048]{2,1,0:T(8,128)(2,1)} %bitcast.128), kind=kLoop, calls=%fused_computation.102 | loop fusion | bytes 4194304 | tf_op jit(solution)/shard_map/slice | solution.py:103
  (53 shorter events, 27.3 us)
Async XLA Ops:
  0.0 27.6 %copy-start = (bf16[64,2048]{1,0:T(8,128)(2,1)S(1)}, bf16[64,2048]{1,0:T(8,128)(2,1)}, u32[]{:S(2)}) copy-start(bf16[64,2048]{1,0:T(8,128)(2,1)} %param.8) | copy-start | bytes 786436
  8.0 32.8 %all-to-all-start = ((bf16[128,5,1]{1,2,0:T(2,128)(2,1)}), bf16[128,5,1]{1,2,0:T(2,128)(2,1)S(1)}, u32[]{:S(2)}, u32[]{:S(2)}) async-start(bf16[128,5,1]{1,2,0:T(2,128)(2,1)} %all_to_all.27), calls=%async_computation | async-start | bytes 131072 | tf_op jit(solution)/shard_map/all_to_all | solution.py:63
  34.9 17.9 %copy-start.2 = (bf16[1,2,192,2048]{3,2,1,0:T(8,128)(2,1)S(1)}, bf16[1,2,192,2048]{3,2,1,0:T(8,128)(2,1)}, u32[]{:S(2)}) copy-start(bf16[1,2,192,2048]{3,2,1,0:T(8,128)(2,1)} %param.12) | copy-start | bytes 4718596
  40.8 444.1 %all-to-all-start.1 = ((bf16[128,5,2048]{2,1,0:T(8,128)(2,1)}), bf16[128,5,2048]{2,1,0:T(8,128)(2,1)}, u32[]{:S(2)}, u32[]{:S(2)}) async-start(bf16[128,5,2048]{2,1,0:T(8,128)(2,1)} %all_to_all.22), calls=%async_computation.1 | async-start | bytes 8388608 | tf_op jit(solution)/shard_map/all_to_all | solution.py:62
  52.7 213.7 %collective-permute-start = (bf16[1,2,192,2048]{3,2,0,1:T(8,128)(2,1)S(1)}, bf16[1,2,192,2048]{3,2,0,1:T(8,128)(2,1)}, u32[]{:S(2)}, u32[]{:S(2)}) collective-permute-start(bf16[1,2,192,2048]{3,2,0,1:T(8,128)(2,1)S(1)} %bitcast.130), channel_id=1, source_target_pairs={{0,4},{4,0},{8,12},{12,8},{16,20},{20,16},{24,28},{28,24},{32,36},... | collective-permute-start | bytes 4718600 | tf_op jit(solution)/shard_map/ppermute | solution.py:17
  56.1 215.9 %copy-start.3 = (bf16[1,192,2048]{2,1,0:T(8,128)(2,1)S(1)}, bf16[1,192,2048]{2,1,0:T(8,128)(2,1)}, u32[]{:S(2)}) copy-start(bf16[1,192,2048]{2,1,0:T(8,128)(2,1)} %param.13) | copy-start | bytes 2359300
  269.7 208.0 %collective-permute-start.1 = (bf16[2,2,192,2048]{3,2,0,1:T(8,128)(2,1)S(1)}, bf16[2,2,192,2048]{3,2,0,1:T(8,128)(2,1)}, u32[]{:S(2)}, u32[]{:S(2)}) collective-permute-start(bf16[2,2,192,2048]{3,2,0,1:T(8,128)(2,1)S(1)} %maximum_select_fusion.1), channel_id=1, source_target_pairs={{0,8},{8,0},{4,12},{12,4},{16,24},{24,16},{20,28},{28,20},{32,40},... | collective-permute-start | bytes 9437192 | tf_op jit(solution)/shard_map/ppermute | solution.py:17
  272.0 84.9 %collective-permute-start.2 = (bf16[1,192,2048]{2,1,0:T(8,128)(2,1)S(1)}, bf16[1,192,2048]{2,1,0:T(8,128)(2,1)S(1)}, u32[]{:S(2)}, u32[]{:S(2)}) collective-permute-start(bf16[1,192,2048]{2,1,0:T(8,128)(2,1)S(1)} %copy-done.3), channel_id=1, source_target_pairs={{0,4},{4,0},{8,12},{12,8},{16,20},{20,16},{24,28},{28,24},{32,36},... | collective-permute-start | bytes 2359304 | tf_op jit(solution)/shard_map/ppermute | solution.py:17
  358.4 115.1 %collective-permute-start.3 = (bf16[2,192,2048]{2,1,0:T(8,128)(2,1)}, bf16[2,192,2048]{2,1,0:T(8,128)(2,1)}, u32[]{:S(2)}, u32[]{:S(2)}) collective-permute-start(bf16[2,192,2048]{2,1,0:T(8,128)(2,1)} %maximum_select_fusion.3), channel_id=1, source_target_pairs={{0,8},{8,0},{4,12},{12,4},{16,24},{24,16},{20,28},{28,20},{32,40},... | collective-permute-start | bytes 4718600 | tf_op jit(solution)/shard_map/ppermute | solution.py:17
  558.4 20.5 %copy-start.4 = (f32[64,8]{0,1:T(8,128)S(1)}, f32[64,8]{0,1:T(8,128)}, u32[]{:S(2)}) copy-start(f32[64,8]{0,1:T(8,128)} %param.9) | copy-start | bytes 6148
  558.4 209.8 %all-to-all-start.2 = ((bf16[128,5,2048]{2,1,0:T(8,128)(2,1)}), bf16[128,5,2048]{2,1,0:T(8,128)(2,1)}, u32[]{:S(2)}, u32[]{:S(2)}) async-start(bf16[128,5,2048]{2,1,0:T(8,128)(2,1)} %broadcast_select_fusion), calls=%async_computation.2 | async-start | bytes 8388608 | tf_op jit(solution)/shard_map/all_to_all | solution.py:99
  775.8 14.8 %copy-start.1 = (bf16[64,2048]{1,0:T(8,128)(2,1)S(1)}, bf16[64,2048]{1,0:T(8,128)(2,1)}, u32[]{:S(2)}) copy-start(bf16[64,2048]{1,0:T(8,128)(2,1)} %param.8) | copy-start | bytes 786436
where the time goes:
time: 791 us
  waiting for transfers between devices  598 us (76%)
  starting transfers between devices  62.1 us (8%)
  local copies, waits for them, and re-layouts  59.8 us (8%)
  matrix products  45.6 us (6%)
  other arithmetic  23.5 us (3%)
    ppermute x4, waiting for transfers between devices, from_partner(): return lax.ppermute(block, axis, route)  403 us
    all_to_all x1, waiting for transfers between devices, local(): lax.all_to_all(back_rows, 'ep', split_axis=0, concat_axis=0, tiled=True)  189 us
    dot_general x5, matrix products, compute_block(): jnp.einsum('rjf,jfd->rd', hidden, pieces_out, preferred_element_type=jnp....  26.6 us
    all_to_all x1, starting transfers between devices, local(): lax.all_to_all(back_rows, 'ep', split_axis=0, concat_axis=0, tiled=True)  20.5 us
    all_to_all x1, starting transfers between devices, local(): lax.all_to_all(send_flag, 'ep', split_axis=0, concat_axis=0, tiled=True)  19.5 us
    dot_general x5, matrix products, compute_block(): jnp.einsum('rd,jfd->rjf', block_rows, gate_weights, preferred_element_typ...  19 us
  transfers between devices with their start and end apart: 7, of which 5 were waited for; matrix products, arithmetic and copies ran while one was open for 3% of the time, Pallas kernels for 0%

commit v1 on v0

v1 whole, which is shorter than its diff:
```python
import functools

import jax
import jax.numpy as jnp
from jax import lax
from jax.experimental import pallas as pl
from jax.experimental.pallas import tpu as pltpu
from jax.sharding import PartitionSpec as P

MESH = pl.DeviceIdType.MESH
GROUP = 4
CAPE = 20
Z = 16
X = 4
Y = 2
RING = Z // 2
COLS = X * Y


def z_place():
    me = lax.axis_index("ep")
    z = me % Z
    return me - z, z


def neighbours():
    base, z = z_place()
    return base + (z + 2) % Z, base + (z + Z - 2) % Z


def signal_all(devices):
    barrier = pltpu.get_barrier_semaphore()
    for device in devices:
        pl.semaphore_signal(barrier, inc=1, device_id={"ep": device}, device_id_type=MESH)
    pl.semaphore_wait(barrier, len(devices))


def gather_kernel(tok_ref, meta_ref, out_ref, mout_ref, local_sem, send_sem, recv_sem):
    base, z = z_place()
    m = z // 2
    ends = neighbours()
    half = tok_ref.shape[0] // 2
    signal_all(ends)
    own = pltpu.make_async_copy(tok_ref, out_ref.at[m], local_sem.at[0])
    own_meta = pltpu.make_async_copy(meta_ref, mout_ref.at[m], local_sem.at[1])
    own.start()
    own_meta.start()

    def copy(way, step, chunk):
        owner = (m + (RING - step if way == 0 else step)) % RING
        if chunk == 2:
            src = meta_ref if step == 0 else mout_ref.at[owner]
            dst = mout_ref.at[owner]
        else:
            rows = pl.ds(chunk * half, half)
            src = tok_ref.at[rows] if step == 0 else out_ref.at[owner, rows]
            dst = out_ref.at[owner, rows]
        return pltpu.make_async_remote_copy(
            src_ref=src,
            dst_ref=dst,
            send_sem=send_sem.at[way, step, chunk],
            recv_sem=recv_sem.at[way, step, chunk],
            device_id={"ep": ends[way]},
            device_id_type=MESH,
        )

    last = RING // 2 - 1
    started, unread = [], {}
    for step in range(last + 1):
        for chunk in (2, 0, 1):
            for way in (0, 1):
                if step == last and way != (0 if chunk in (0, 2) else 1):
                    continue
                if step > 0:
                    unread.pop((way, step - 1, chunk)).wait_recv()
                sent = copy(way, step, chunk)
                sent.start()
                started.append(sent)
                unread[way, step, chunk] = sent
    for sent in unread.values():
        sent.wait_recv()
    for sent in started:
        sent.wait_send()
    own.wait()
    own_meta.wait()


def z_gather(tokens, meta):
    rows, width = tokens.shape
    return pl.pallas_call(
        gather_kernel,
        out_shape=(
            jax.ShapeDtypeStruct((RING, rows, width), tokens.dtype),
            jax.ShapeDtypeStruct((RING,) + meta.shape, meta.dtype),
        ),
        in_specs=[pl.BlockSpec(memory_space=pl.ANY)] * 2,
        out_specs=[pl.BlockSpec(memory_space=pl.ANY)] * 2,
        scratch_shapes=[
            pltpu.SemaphoreType.DMA((2,)),
            pltpu.SemaphoreType.DMA((2, RING // 2, 3)),
            pltpu.SemaphoreType.DMA((2, RING // 2, 3)),
        ],
        compiler_params=pltpu.CompilerParams(collective_id=0, has_side_effects=True),
        name="z_gather",
    )(tokens, meta)


def columns():
    me = lax.axis_index("ep")
    y, x, z = me // (X * Z), me // Z % X, me % Z
    others = []
    for ky in range(Y):
        for kx in range(X):
            if kx or ky:
                others.append(((y + ky) % Y) * X + (x + kx) % X)
    return y * X + x, z, others


def exchange(send_ref, recv_ref, local_sem, send_sem, recv_sem):
    mine, z, others = columns()
    own = pltpu.make_async_copy(send_ref.at[mine], recv_ref.at[mine], local_sem.at[0])
    own.start()
    copies = []
    for k, other in enumerate(others):
        copies.append(
            pltpu.make_async_remote_copy(
                src_ref=send_ref.at[other],
                dst_ref=recv_ref.at[mine],
                send_sem=send_sem.at[k],
                recv_sem=recv_sem.at[k],
                device_id={"ep": other * Z + z},
                device_id_type=MESH,
            )
        )
    for sent in copies:
        sent.start()
    return own, copies


def out_kernel(
    send_ref, win_ref, wout_ref, recv_ref, win2_ref, wout2_ref,
    local_sem, send_sem, recv_sem, wlocal_sem, wsend_sem, wrecv_sem,
):
    mine, z, others = columns()
    member = z % 2
    partner = mine * Z + z + 1 - 2 * member
    signal_all([other * Z + z for other in others] + [partner])
    own, copies = exchange(send_ref, recv_ref, local_sem, send_sem, recv_sem)
    pieces = [
        (win_ref.at[0, 0], win2_ref.at[0, member]),
        (win_ref.at[0, 1], win2_ref.at[1, member]),
        (wout_ref.at[0], wout2_ref.at[member]),
    ]
    kept = []
    for k, (src, dst) in enumerate(pieces):
        copies.append(
            pltpu.make_async_remote_copy(
                src_ref=src,
                dst_ref=dst,
                send_sem=wsend_sem.at[k],
                recv_sem=wrecv_sem.at[k],
                device_id={"ep": partner},
                device_id_type=MESH,
            )
        )
        copies[-1].start()
        kept.append(pltpu.make_async_copy(src, dst, wlocal_sem.at[k]))
        kept[-1].start()
    for sent in copies:
        sent.wait()
    own.wait()
    for piece in kept:
        piece.wait()


def xy_out(send, w_in, w_out):
    _, two, ff, width = w_in.shape
    return pl.pallas_call(
        out_kernel,
        out_shape=(
            jax.ShapeDtypeStruct(send.shape, send.dtype),
            jax.ShapeDtypeStruct((two, 2, ff, width), w_in.dtype),
            jax.ShapeDtypeStruct((2, ff, width), w_out.dtype),
        ),
        in_specs=[pl.BlockSpec(memory_space=pl.ANY)] * 3,
        out_specs=[pl.BlockSpec(memory_space=pl.ANY)] * 3,
        scratch_shapes=[
            pltpu.SemaphoreType.DMA((1,)),
            pltpu.SemaphoreType.DMA((COLS - 1,)),
            pltpu.SemaphoreType.DMA((COLS - 1,)),
            pltpu.SemaphoreType.DMA((3,)),
            pltpu.SemaphoreType.DMA((3,)),
            pltpu.SemaphoreType.DMA((3,)),
        ],
        compiler_params=pltpu.CompilerParams(collective_id=1, has_side_effects=True),
        name="xy_out",
    )(send, w_in, w_out)


def back_kernel(send_ref, recv_ref, local_sem, send_sem, recv_sem):
    mine, z, others = columns()
    signal_all([other * Z + z for other in others])
    own, copies = exchange(send_ref, recv_ref, local_sem, send_sem, recv_sem)
    for sent in copies:
        sent.wait()
    own.wait()


def xy_back(send):
    return pl.pallas_call(
        back_kernel,
        out_shape=jax.ShapeDtypeStruct(send.shape, send.dtype),
        in_specs=[pl.BlockSpec(memory_space=pl.ANY)],
        out_specs=pl.BlockSpec(memory_space=pl.ANY),
        scratch_shapes=[
            pltpu.SemaphoreType.DMA((1,)),
            pltpu.SemaphoreType.DMA((COLS - 1,)),
            pltpu.SemaphoreType.DMA((COLS - 1,)),
        ],
        compiler_params=pltpu.CompilerParams(collective_id=2, has_side_effects=True),
        name="xy_back",
    )(send)


def reduce_kernel(part_ref, out_ref, come, go, send_sem, recv_sem):
    base, z = z_place()
    m = z // 2
    ends = neighbours()
    half = out_ref.shape[0] // 2
    signal_all(ends)
    last = RING // 2 - 1

    def copy(way, step, chunk):
        rows = pl.ds(chunk * half, half)
        return pltpu.make_async_remote_copy(
            src_ref=go.at[way, step, rows],
            dst_ref=come.at[way, step, rows],
            send_sem=send_sem.at[way, step, chunk],
            recv_sem=recv_sem.at[way, step, chunk],
            device_id={"ep": ends[way]},
            device_id_type=MESH,
        )

    started, unread = [], {}
    for step in range(last + 1):
        for chunk in (0, 1):
            for way in (0, 1):
                if step == 0 and way != chunk:
                    continue
                ahead = RING // 2 - step
                target = (m + (ahead if way == 0 else RING - ahead)) % RING
                rows = pl.ds(chunk * half, half)
                value = part_ref[target, rows]
                earlier = unread.pop((way, step - 1, chunk), None)
                if earlier is not None:
                    earlier.wait_recv()
                    value = (
                        value.astype(jnp.float32) + come[way, step - 1, rows].astype(jnp.float32)
                    ).astype(jnp.bfloat16)
                go[way, step, rows] = value
                sent = copy(way, step, chunk)
                sent.start()
                started.append(sent)
                unread[way, step, chunk] = sent
    for chunk in (0, 1):
        rows = pl.ds(chunk * half, half)
        total = part_ref[m, rows].astype(jnp.float32)
        for way in (0, 1):
            unread.pop((way, last, chunk)).wait_recv()
            total += come[way, last, rows].astype(jnp.float32)
        out_ref[rows] = total.astype(jnp.bfloat16)
    for sent in started:
        sent.wait_send()


def z_reduce(part):
    _, rows, width = part.shape
    return pl.pallas_call(
        reduce_kernel,
        out_shape=jax.ShapeDtypeStruct((rows, width), part.dtype),
        in_specs=[pl.BlockSpec(memory_space=pltpu.VMEM)],
        out_specs=pl.BlockSpec(memory_space=pltpu.VMEM),
        scratch_shapes=[
            pltpu.VMEM((2, RING // 2, rows, width), part.dtype),
            pltpu.VMEM((2, RING // 2, rows, width), part.dtype),
            pltpu.SemaphoreType.DMA((2, RING // 2, 2)),
            pltpu.SemaphoreType.DMA((2, RING // 2, 2)),
        ],
        compiler_params=pltpu.CompilerParams(
            collective_id=3, has_side_effects=True, vmem_limit_bytes=32 << 20
        ),
        name="z_reduce",
    )(part)


def local(tokens, gates, expert_ids, slot_expert, w_in, w_out):
    rows, width = tokens.shape
    top = expert_ids.shape[1]
    meta = jnp.concatenate([expert_ids.astype(jnp.float32), gates], axis=1)
    meta = meta.reshape(rows * 2 * top // 128, 128)
    all_tokens, all_meta = z_gather(tokens, meta)
    all_meta = all_meta.reshape(RING * rows, 2 * top)
    ids, weights = all_meta[:, :top], all_meta[:, top:]
    z_block = lax.axis_index("ep") % Z // GROUP
    here = lax.dynamic_index_in_dim(
        slot_expert.reshape(COLS, Z // GROUP), z_block, 1, keepdims=False
    ).astype(jnp.float32)
    same = ids[None, :, :] == here[:, None, None]
    gate = jnp.sum(jnp.where(same, weights[None], 0.0), axis=2)
    chosen = jnp.any(same, axis=2)
    before = jnp.tril(jnp.ones((rows, rows), jnp.bfloat16), -1)
    rank = jnp.einsum(
        "cbs,ts->cbt",
        chosen.reshape(COLS, RING, rows).astype(jnp.bfloat16),
        before,
        preferred_element_type=jnp.float32,
    ).astype(jnp.int32)
    slot = rank + CAPE * jnp.arange(RING, dtype=jnp.int32)[None, :, None]
    slot = jnp.where(chosen, slot.reshape(COLS, RING * rows), -1)
    slots = RING * CAPE
    hit = jnp.arange(slots, dtype=jnp.int32)[None, :, None] == slot[:, None, :]
    pick = hit.astype(jnp.bfloat16).reshape(COLS * slots, RING * rows)
    send = jnp.dot(
        pick, all_tokens.reshape(RING * rows, width), preferred_element_type=jnp.float32
    ).astype(jnp.bfloat16)
    recv, win2, wout2 = xy_out(send.reshape(COLS, slots, width), w_in, w_out)
    recv = recv.reshape(COLS * slots, width)
    ff = win2.shape[1] * win2.shape[2]
    both = lax.dot_general(
        recv,
        win2.reshape(2 * ff, width),
        (((1,), (1,)), ((), ())),
        preferred_element_type=jnp.float32,
    )
    hidden = (jax.nn.silu(both[:, :ff]) * both[:, ff:]).astype(jnp.bfloat16)
    produced = jnp.dot(
        hidden, wout2.reshape(ff, width), preferred_element_type=jnp.float32
    ).astype(jnp.bfloat16)
    back = xy_back(produced.reshape(COLS, slots, width)).reshape(COLS * slots, width)
    high = lax.reduce_precision(gate, 8, 7)
    low = gate - high
    zero = jnp.zeros((), jnp.float32)
    part = jnp.zeros((RING * rows, width), jnp.float32)
    for piece in (high, low):
        mix = jnp.where(hit, piece[:, None, :], zero).astype(jnp.bfloat16)
        part += lax.dot_general(
            mix.reshape(COLS * slots, RING * rows),
            back,
            (((0,), (0,)), ((), ())),
            preferred_element_type=jnp.float32,
        )
    return z_reduce(part.astype(jnp.bfloat16).reshape(RING, rows, width))


def solution(mesh):
    return jax.shard_map(
        local,
        mesh=mesh,
        in_specs=(
            P(("dp", "ep"), None),
            P(("dp", "ep"), None),
            P(("dp", "ep"), None),
            P("dp"),
            P(("dp", "ep"), None, None, None),
            P(("dp", "ep"), None, None),
        ),
        out_specs=P(("dp", "ep"), None),
        check_vma=False,
    )
```

time: 791 us -> 317 us (0.40)
  the two profiles are of different devices: /device:TPU:66 before, /device:TPU:44 now
where the time goes in v1:
time: 317 us; the launch traced here: 316 us
  Pallas kernels  285 us (90%)
  matrix products  25 us (8%)
  local copies, waits for them, and re-layouts  3.74 us (1%)
    pallas_call x1, Pallas kernels, xy_out(): pl.pallas_call(out_kernel, out_shape=(jax.ShapeDtypeStruct(send.shape, se...  94.6 us
    pallas_call x1, Pallas kernels, xy_back(): pl.pallas_call(back_kernel, out_shape=jax.ShapeDtypeStruct(send.shape, se...  92.4 us
    pallas_call x1, Pallas kernels, z_gather(): pl.pallas_call(gather_kernel, out_shape=(jax.ShapeDtypeStruct((RING, rows...  53.3 us
    pallas_call x1, Pallas kernels, z_reduce(): pl.pallas_call(reduce_kernel, out_shape=jax.ShapeDtypeStruct((rows, width...  44.5 us
    dot_general x2, matrix products, local(): lax.dot_general(mix.reshape(COLS * slots, RING * rows), back, (((0,), (0,...  8.15 us
    dot_general x1, matrix products, local(): lax.dot_general(recv, win2.reshape(2 * ff, width), (((1,), (1,)), ((), ()...  7.31 us

profile of v1, /device:TPU:44, one launch (start us, length us, event | category | flops | bytes accessed | tf_op | source)
XLA Modules:
  0.0 315.8 jit_solution(10146399543199909846)
XLA Ops:
  0.0 0.7 convert_element_type.36
  0.7 0.7 pad_maximum_fusion
  1.4 0.7 reshape.100
  2.1 0.2 convert_reduce_fusion
  2.3 0.1 copy.9
  2.4 0.7 reshape.98.meta_ref
  3.1 53.3 %z_gather.1 = (bf16[8,64,2048]{2,1,0:T(8,128)(2,1)}, f32[8,8,128]{2,1,0:T(8,128)}) custom-call(bf16[64,2048]{1,0:T(8,128)(2,1)} %tok_ref.1, f32[8,128]{1,0:T(8,128)} %reshape.98.meta_ref), custom_call_target="tpu_custom_call" | custom-call | tf_op jit(solution)/shard_map/z_gather/pallas_call | solution.py:90
  56.4 0.0 copy-start.1
  56.4 1.0 reshape.99
  57.4 0.1 fusion.24
  57.6 0.1 copy.11
  57.7 0.1 copy.10
  57.8 0.1 fusion.12
  57.9 0.1 compare_reduce_fusion
  58.0 0.1 reshape.101
  58.1 0.2 fusion.9
  58.3 0.1 reshape.102
  58.4 0.4 iota_compare_fusion
  58.8 0.0 copy-done.1
  58.8 4.6 %convolution_convert_fusion.1 = bf16[1280,2048]{1,0:T(8,128)(2,1)} fusion(pred[1280,512]{1,0:T(32,128)(4,1)S(1)} %bitcast.28, bf16[512,2048]{1,0:T(8,128)(2,1)S(1)} %bitcast.31), kind=kOutput, calls=%fused_computation.1 | convolution fusion | flops 2686976000 | bytes 7995392 | tf_op jit(solution)/shard_map/dot_general | solution.py:323
  63.4 94.6 %xy_out.1 = (bf16[8,160,2048]{2,1,0:T(8,128)(2,1)}, bf16[2,2,192,2048]{3,2,1,0:T(8,128)(2,1)}, bf16[2,192,2048]{2,1,0:T(8,128)(2,1)}) custom-call(bf16[8,160,2048]{2,1,0:T(8,128)(2,1)} %bitcast.27, bf16[1,2,192,2048]{3,2,1,0:T(8,128)(2,1)} %win_ref.1, bf16[1,192,2048]{2,1,0:T(8,128)(2,1)} %wout_ref.1), custom_call_target="tpu_custom_call" | custom-call | tf_op jit(solution)/shard_map/xy_out/pallas_call | solution.py:178
  158.0 0.0 copy-start.2
  158.0 7.3 %fusion.25 = f32[1280,768]{1,0:T(8,128)S(1)} fusion(bf16[1280,2048]{1,0:T(8,128)(2,1)} %bitcast.29, bf16[768,2048]{1,0:T(8,128)(2,1)} %bitcast.30), kind=kOutput, calls=%fused_computation.40 | convolution fusion | flops 4026531840 | bytes 12320768 | tf_op jit(solution)/shard_map/dot_general | solution.py:329
  165.4 0.0 copy-done.2
  165.4 4.7 %convolution_convert_fusion = bf16[1280,2048]{1,0:T(8,128)(2,1)} fusion(bf16[384,2048]{1,0:T(8,128)(2,1)S(1)} %bitcast.32, f32[1280,768]{1,0:T(8,128)S(1)} %fusion.25), kind=kOutput, calls=%fused_computation | convolution fusion | flops 2018836480 | bytes 10747904 | tf_op jit(solution)/shard_map/dot_general | solution.py:336
  170.1 92.4 %xy_back.1 = bf16[8,160,2048]{2,1,0:T(8,128)(2,1)} custom-call(bf16[8,160,2048]{2,1,0:T(8,128)(2,1)} %bitcast.26), custom_call_target="tpu_custom_call" | custom-call | tf_op jit(solution)/shard_map/xy_back/pallas_call | solution.py:210
  262.4 0.0 copy-start
  262.4 5.0 %fusion.2 = f32[512,2048,1]{1,0,2:T(8,128)S(1)} fusion(bf16[8,160,2048]{2,1,0:T(8,128)(2,1)} %xy_back.1, bf16[8,512]{1,0:T(8,128)(2,1)S(1)} %get-tuple-element.18, s32[8,512]{1,0:T(8,128)S(1)} %broadcast_select_fusion), kind=kOutput, calls=%fused_computation.9 | convolution fusion | flops 2685665280 | bytes 9461760 | tf_op jit(solution)/shard_map/dot_general | solution.py:346
  267.5 0.0 copy-done
  267.5 3.1 fusion
  270.6 44.5 %z_reduce.1 = bf16[64,2048]{1,0:T(8,128)(2,1)S(1)} custom-call(bf16[8,64,2048]{2,1,0:T(8,128)(2,1)S(1)} %bitcast.25), custom_call_target="tpu_custom_call" | custom-call | tf_op jit(solution)/shard_map/z_reduce/pallas_call | solution.py:278
  315.1 0.7 copy.15
  (4 shorter events, 0.0 us)
Async XLA Ops:
  56.4 2.4 copy-start.1
  158.0 7.3 %copy-start.2 = (bf16[2,192,2048]{2,1,0:T(8,128)(2,1)S(1)}, bf16[2,192,2048]{2,1,0:T(8,128)(2,1)}, u32[]{:S(2)}) copy-start(bf16[2,192,2048]{2,1,0:T(8,128)(2,1)} %get-tuple-element.14) | copy-start | bytes 4718596
  262.4 5.0 %copy-start = (bf16[8,160,2048]{2,1,0:T(8,128)(2,1)S(1)}, bf16[8,160,2048]{2,1,0:T(8,128)(2,1)}, u32[]{:S(2)}) copy-start(bf16[8,160,2048]{2,1,0:T(8,128)(2,1)} %xy_back.1) | copy-start | bytes 15728644

commit v2 on v1

v2 whole, which is shorter than its diff:
```python
import jax
import jax.numpy as jnp
from jax import lax
from jax.experimental import pallas as pl
from jax.experimental.pallas import tpu as pltpu
from jax.sharding import PartitionSpec as P

MESH = pl.DeviceIdType.MESH
GROUP = 4
CAPE = 20
Z = 16
X = 4
Y = 2
RING = Z // 2
COLS = X * Y
CHUNKS = 4


def z_place():
    me = lax.axis_index("ep")
    z = me % Z
    return me - z, z


def neighbours():
    base, z = z_place()
    return base + (z + 2) % Z, base + (z + Z - 2) % Z


def signal_all(devices):
    barrier = pltpu.get_barrier_semaphore()
    for device in devices:
        pl.semaphore_signal(barrier, inc=1, device_id={"ep": device}, device_id_type=MESH)
    pl.semaphore_wait(barrier, len(devices))


def columns():
    me = lax.axis_index("ep")
    return me // (X * Z), me // Z % X, me % Z


def column_at(y, x):
    return y % Y * X + x % X


def xy_peers():
    y, x, z = columns()
    return [
        column_at(y + ky, x + kx) * Z + z for ky in range(Y) for kx in range(X) if kx or ky
    ]


def xy_copies(send_ref, recv_ref, relay_ref, cols, send_sem, recv_sem):
    y, x, z = columns()
    mine = column_at(y, x)
    half = send_ref.shape[1] // 2

    def remote(k, src, dst, column):
        return pltpu.make_async_remote_copy(
            src_ref=src,
            dst_ref=dst,
            send_sem=send_sem.at[k],
            recv_sem=recv_sem.at[k],
            device_id={"ep": column * Z + z},
            device_id_type=MESH,
        )

    relays, forwards, direct = [], [], []
    for way, step in ((0, 1), (1, X - 1)):
        rows = pl.ds(way * half, half)
        for ky in range(Y):
            k = 2 * way + ky
            slot = relay_ref.at[way, ky, :, cols]
            relays.append(
                remote(
                    k, send_ref.at[column_at(y + ky, x + 2), rows, cols], slot, column_at(y, x + step)
                )
            )
            forwards.append(
                remote(
                    4 + k,
                    slot,
                    recv_ref.at[column_at(y, x + X - step), rows, cols],
                    column_at(y + ky, x + step),
                )
            )
    for k, (ky, kx) in enumerate(((1, 1), (1, 3), (1, 0), (0, 1), (0, 3))):
        other = column_at(y + ky, x + kx)
        direct.append(
            remote(8 + k, send_ref.at[other, :, cols], recv_ref.at[mine, :, cols], other)
        )
    return relays, forwards, direct


XY_COPIES = 13


def out_kernel(
    tok_ref, ids_ref, gates_ref, expert_ref, win_ref, wout_ref,
    recv_ref, meta_ref, win2_ref, wout2_ref,
    held, table, pick, send, relay,
    own_sem, zs_sem, zr_sem, ms_sem, mr_sem, xs_sem, xr_sem, keep_sem, ws_sem, wr_sem, wl_sem,
):
    base, z = z_place()
    m, member = z // 2, z % 2
    ends = neighbours()
    rows, width = tok_ref.shape
    slots = pick.shape[1]
    part = width // CHUNKS
    y, x, _ = columns()
    mine = column_at(y, x)
    partner = mine * Z + z + 1 - 2 * member
    ring = [base + (z + 2 * k) % Z for k in range(1, RING)]
    signal_all(ring + [partner] + xy_peers())

    own = pltpu.make_async_copy(tok_ref, held.at[pl.ds(m * rows, rows)], own_sem.at[0])
    own.start()
    last = RING // 2 - 1
    z_sent, started = {}, []

    def z_copy(way, step, chunk):
        owner = (m + (RING - step if way == 0 else step)) % RING
        count = rows // 2 if step == last else rows
        first = way * (rows // 2) if step == last else 0
        cols = pl.ds(chunk * part, part)
        there = held.at[pl.ds(owner * rows + first, count), cols]
        return pltpu.make_async_remote_copy(
            src_ref=tok_ref.at[:, cols] if step == 0 else there,
            dst_ref=there,
            send_sem=zs_sem.at[way, step, chunk],
            recv_sem=zr_sem.at[way, step, chunk],
            device_id={"ep": ends[way]},
            device_id_type=MESH,
        )

    def z_go(chunk, step):
        for way in (0, 1):
            if step:
                z_sent[way, step - 1, chunk].wait_recv()
            sent = z_copy(way, step, chunk)
            sent.start()
            z_sent[way, step, chunk] = sent
            started.append(sent)

    z_go(0, 0)

    chosen = jnp.zeros((Z // GROUP * COLS, rows), jnp.float32)
    gate = jnp.zeros((Z // GROUP * COLS, rows), jnp.float32)
    for k in range(ids_ref.shape[0]):
        same = ids_ref[pl.ds(k, 1), :] == expert_ref[...]
        chosen += jnp.where(same, 1.0, 0.0)
        gate += jnp.where(same, gates_ref[pl.ds(k, 1), :], 0.0)
    earlier = lax.broadcasted_iota(jnp.int32, (rows, rows), 0) < lax.broadcasted_iota(
        jnp.int32, (rows, rows), 1
    )
    rank = jnp.dot(
        chosen.astype(jnp.bfloat16),
        jnp.where(earlier, 1.0, 0.0).astype(jnp.bfloat16),
        preferred_element_type=jnp.float32,
    )
    slot = jnp.where(chosen > 0.5, rank + (m * CAPE).astype(jnp.float32), -1.0)
    table[:, 0] = jnp.concatenate([slot, slot], axis=1).reshape(Z // GROUP, COLS, 2 * rows)
    table[:, 1] = jnp.concatenate([gate, gate], axis=1).reshape(Z // GROUP, COLS, 2 * rows)
    metas = []
    for k in range(1, RING):
        other = (m + k) % RING
        metas.append(
            pltpu.make_async_remote_copy(
                src_ref=table.at[other // 2],
                dst_ref=meta_ref.at[m],
                send_sem=ms_sem.at[k - 1],
                recv_sem=mr_sem.at[k - 1],
                device_id={"ep": base + (z + 2 * k) % Z},
                device_id_type=MESH,
            )
        )
        metas[-1].start()
    meta_ref[m] = table[m // 2]

    pieces = [
        (win_ref.at[0, 0], win2_ref.at[0, member]),
        (win_ref.at[0, 1], win2_ref.at[1, member]),
        (wout_ref.at[0], wout2_ref.at[member]),
    ]
    weights, kept = [], []
    exchanges = []
    for chunk in range(CHUNKS):
        cols = pl.ds(chunk * part, part)
        z_go(chunk, 1)
        z_go(chunk, 2)
        if chunk + 1 < CHUNKS:
            z_go(chunk + 1, 0)
        z_go(chunk, 3)
        if chunk == 0:
            for sent in metas:
                sent.wait_recv()
            for pair in range(RING // 2):
                left = lax.broadcasted_iota(jnp.int32, (COLS, 2 * rows), 1) < rows
                both = jnp.where(left, meta_ref[2 * pair, 0], meta_ref[2 * pair + 1, 0])
                place = lax.broadcasted_iota(jnp.int32, (slots, 2 * rows), 0).astype(jnp.float32)
                for column in range(COLS):
                    hit = place == jnp.broadcast_to(both[column : column + 1], place.shape)
                    pick[column, :, pl.ds(pair * 2 * rows, 2 * rows)] = jnp.where(
                        hit, 1.0, 0.0
                    ).astype(jnp.bfloat16)
            own.wait()
        else:
            relays, forwards, _ = exchanges[chunk - 1]
            for came, sent in zip(relays, forwards):
                came.wait_recv()
                sent.start()
        for way in (0, 1):
            z_sent[way, last, chunk].wait_recv()

        @pl.loop(0, COLS)
        def _(column):
            send[column, :, cols] = jnp.dot(
                pick[column], held[:, cols], preferred_element_type=jnp.float32
            ).astype(jnp.bfloat16)

        relays, forwards, direct = xy_copies(
            send, recv_ref, relay, cols, xs_sem.at[chunk], xr_sem.at[chunk]
        )
        for sent in relays + direct:
            sent.start()
        exchanges.append((relays, forwards, direct))
        kept.append(
            pltpu.make_async_copy(
                send.at[mine, :, cols], recv_ref.at[mine, :, cols], keep_sem.at[chunk]
            )
        )
        kept[-1].start()
        if chunk:
            k = chunk - 1
            src, dst = pieces[k]
            weights.append(
                pltpu.make_async_remote_copy(
                    src_ref=src,
                    dst_ref=dst,
                    send_sem=ws_sem.at[k],
                    recv_sem=wr_sem.at[k],
                    device_id={"ep": partner},
                    device_id_type=MESH,
                )
            )
            weights[-1].start()
            kept.append(pltpu.make_async_copy(src, dst, wl_sem.at[k]))
            kept[-1].start()
    relays, forwards, _ = exchanges[-1]
    for came, sent in zip(relays, forwards):
        came.wait_recv()
        sent.start()
    for relays, forwards, direct in exchanges:
        for sent in direct + forwards:
            sent.wait_recv()
        for sent in relays + forwards + direct:
            sent.wait_send()
    for sent in started + metas:
        sent.wait_send()
    for sent in weights:
        sent.wait()
    for piece in kept:
        piece.wait()


def dispatch(tokens, ids, gates, expert, w_in, w_out):
    rows, width = tokens.shape
    _, two, ff, _ = w_in.shape
    slots = RING * CAPE
    steps = RING // 2
    dma = pltpu.SemaphoreType.DMA
    return pl.pallas_call(
        out_kernel,
        out_shape=(
            jax.ShapeDtypeStruct((COLS, slots, width), tokens.dtype),
            jax.ShapeDtypeStruct((RING, 2, COLS, 2 * rows), jnp.float32),
            jax.ShapeDtypeStruct((two, 2, ff, width), w_in.dtype),
            jax.ShapeDtypeStruct((2, ff, width), w_out.dtype),
        ),
        in_specs=[pl.BlockSpec(memory_space=pl.ANY)]
        + [pl.BlockSpec(memory_space=pltpu.VMEM)] * 3
        + [pl.BlockSpec(memory_space=pl.ANY)] * 2,
        out_specs=[
            pl.BlockSpec(memory_space=pl.ANY),
            pl.BlockSpec(memory_space=pltpu.VMEM),
            pl.BlockSpec(memory_space=pl.ANY),
            pl.BlockSpec(memory_space=pl.ANY),
        ],
        scratch_shapes=[
            pltpu.VMEM((RING * rows, width), tokens.dtype),
            pltpu.VMEM((Z // GROUP, 2, COLS, 2 * rows), jnp.float32),
            pltpu.VMEM((COLS, slots, RING * rows), jnp.bfloat16),
            pltpu.VMEM((COLS, slots, width), tokens.dtype),
            pltpu.VMEM((2, Y, slots // 2, width), tokens.dtype),
            dma((1,)),
            dma((2, steps, CHUNKS)),
            dma((2, steps, CHUNKS)),
            dma((RING - 1,)),
            dma((RING - 1,)),
            dma((CHUNKS, XY_COPIES)),
            dma((CHUNKS, XY_COPIES)),
            dma((CHUNKS,)),
            dma((3,)),
            dma((3,)),
            dma((3,)),
        ],
        compiler_params=pltpu.CompilerParams(
            collective_id=1, has_side_effects=True, vmem_limit_bytes=40 << 20
        ),
        name="dispatch",
    )(tokens, ids, gates, expert, w_in, w_out)


def back_kernel(send_ref, recv_ref, relay, local_sem, send_sem, recv_sem):
    y, x, _ = columns()
    mine = column_at(y, x)
    signal_all(xy_peers())
    own = pltpu.make_async_copy(send_ref.at[mine], recv_ref.at[mine], local_sem.at[0])
    cols = pl.ds(0, send_ref.shape[2])
    relays, forwards, direct = xy_copies(send_ref, recv_ref, relay, cols, send_sem, recv_sem)
    for sent in relays + direct:
        sent.start()
    own.start()
    for came, sent in zip(relays, forwards):
        came.wait_recv()
        sent.start()
    for sent in direct + forwards:
        sent.wait_recv()
    for sent in relays + forwards + direct:
        sent.wait_send()
    own.wait()


def xy_back(send):
    _, slots, width = send.shape
    return pl.pallas_call(
        back_kernel,
        out_shape=jax.ShapeDtypeStruct(send.shape, send.dtype),
        in_specs=[pl.BlockSpec(memory_space=pl.ANY)],
        out_specs=pl.BlockSpec(memory_space=pl.ANY),
        scratch_shapes=[
            pltpu.VMEM((2, Y, slots // 2, width), send.dtype),
            pltpu.SemaphoreType.DMA((1,)),
            pltpu.SemaphoreType.DMA((XY_COPIES,)),
            pltpu.SemaphoreType.DMA((XY_COPIES,)),
        ],
        compiler_params=pltpu.CompilerParams(collective_id=2, has_side_effects=True),
        name="xy_back",
    )(send)


def reduce_kernel(part_ref, out_ref, come, go, send_sem, recv_sem):
    base, z = z_place()
    m = z // 2
    ends = neighbours()
    half = out_ref.shape[0] // 2
    signal_all(ends)
    last = RING // 2 - 1

    def copy(way, step, chunk):
        rows = pl.ds(chunk * half, half)
        return pltpu.make_async_remote_copy(
            src_ref=go.at[way, step, rows],
            dst_ref=come.at[way, step, rows],
            send_sem=send_sem.at[way, step, chunk],
            recv_sem=recv_sem.at[way, step, chunk],
            device_id={"ep": ends[way]},
            device_id_type=MESH,
        )

    started, unread = [], {}
    for step in range(last + 1):
        for chunk in (0, 1):
            for way in (0, 1):
                if step == 0 and way != chunk:
                    continue
                ahead = RING // 2 - step
                target = (m + (ahead if way == 0 else RING - ahead)) % RING
                rows = pl.ds(chunk * half, half)
                value = part_ref[target, rows]
                earlier = unread.pop((way, step - 1, chunk), None)
                if earlier is not None:
                    earlier.wait_recv()
                    value = (
                        value.astype(jnp.float32) + come[way, step - 1, rows].astype(jnp.float32)
                    ).astype(jnp.bfloat16)
                go[way, step, rows] = value
                sent = copy(way, step, chunk)
                sent.start()
                started.append(sent)
                unread[way, step, chunk] = sent
    for chunk in (0, 1):
        rows = pl.ds(chunk * half, half)
        total = part_ref[m, rows].astype(jnp.float32)
        for way in (0, 1):
            unread.pop((way, last, chunk)).wait_recv()
            total += come[way, last, rows].astype(jnp.float32)
        out_ref[rows] = total.astype(jnp.bfloat16)
    for sent in started:
        sent.wait_send()


def z_reduce(part):
    _, rows, width = part.shape
    return pl.pallas_call(
        reduce_kernel,
        out_shape=jax.ShapeDtypeStruct((rows, width), part.dtype),
        in_specs=[pl.BlockSpec(memory_space=pltpu.VMEM)],
        out_specs=pl.BlockSpec(memory_space=pltpu.VMEM),
        scratch_shapes=[
            pltpu.VMEM((2, RING // 2, rows, width), part.dtype),
            pltpu.VMEM((2, RING // 2, rows, width), part.dtype),
            pltpu.SemaphoreType.DMA((2, RING // 2, 2)),
            pltpu.SemaphoreType.DMA((2, RING // 2, 2)),
        ],
        compiler_params=pltpu.CompilerParams(
            collective_id=3, has_side_effects=True, vmem_limit_bytes=32 << 20
        ),
        name="z_reduce",
    )(part)


def local(tokens, gates, expert_ids, slot_expert, w_in, w_out):
    rows, width = tokens.shape
    expert = slot_expert.reshape(COLS, Z // GROUP).T.reshape(-1, 1)
    recv, meta, win2, wout2 = dispatch(tokens, expert_ids.T, gates.T, expert, w_in, w_out)
    slots = RING * CAPE
    recv = recv.reshape(COLS * slots, width)
    ff = win2.shape[1] * win2.shape[2]
    both = lax.dot_general(
        recv,
        win2.reshape(2 * ff, width),
        (((1,), (1,)), ((), ())),
        preferred_element_type=jnp.float32,
    )
    hidden = (jax.nn.silu(both[:, :ff]) * both[:, ff:]).astype(jnp.bfloat16)
    produced = jnp.dot(
        hidden, wout2.reshape(ff, width), preferred_element_type=jnp.float32
    ).astype(jnp.bfloat16)
    back = xy_back(produced.reshape(COLS, slots, width)).reshape(COLS * slots, width)
    meta = meta[..., :rows].transpose(1, 2, 0, 3).reshape(2, COLS, RING * rows)
    slot, gate = meta[0].astype(jnp.int32), meta[1]
    hit = jnp.arange(slots, dtype=jnp.int32)[None, :, None] == slot[:, None, :]
    high = lax.reduce_precision(gate, 8, 7)
    low = gate - high
    zero = jnp.zeros((), jnp.float32)
    part = jnp.zeros((RING * rows, width), jnp.float32)
    for piece in (high, low):
        mix = jnp.where(hit, piece[:, None, :], zero).astype(jnp.bfloat16)
        part += lax.dot_general(
            mix.reshape(COLS * slots, RING * rows),
            back,
            (((0,), (0,)), ((), ())),
            preferred_element_type=jnp.float32,
        )
    return z_reduce(part.astype(jnp.bfloat16).reshape(RING, rows, width))


def solution(mesh):
    return jax.shard_map(
        local,
        mesh=mesh,
        in_specs=(
            P(("dp", "ep"), None),
            P(("dp", "ep"), None),
            P(("dp", "ep"), None),
            P("dp"),
            P(("dp", "ep"), None, None, None),
            P(("dp", "ep"), None, None),
        ),
        out_specs=P(("dp", "ep"), None),
        check_vma=False,
    )
```

time: 317 us -> 252 us (0.79)
  the two profiles are of different devices: /device:TPU:44 before, /device:TPU:10 now
where the time goes in v2:
time: 252 us
  Pallas kernels  228 us (90%)
  matrix products  17.2 us (7%)
  local copies, waits for them, and re-layouts  6.65 us (3%)
    pallas_call x1, Pallas kernels, dispatch(): pl.pallas_call(out_kernel, out_shape=(jax.ShapeDtypeStruct((COLS, slots,...  128 us
    pallas_call x1, Pallas kernels, xy_back(): pl.pallas_call(back_kernel, out_shape=jax.ShapeDtypeStruct(send.shape, se...  59.2 us
    pallas_call x1, Pallas kernels, z_reduce(): pl.pallas_call(reduce_kernel, out_shape=jax.ShapeDtypeStruct((rows, width...  40.2 us
    dot_general x2, matrix products, local(): lax.dot_general(mix.reshape(COLS * slots, RING * rows), back, (((0,), (0,...  8.14 us
    unnamed x15, local copies, waits for them, and re-layouts  5.58 us

profile of v2, /device:TPU:10, one launch (start us, length us, event | category | flops | bytes accessed | tf_op | source)
XLA Modules:
  0.0 251.8 jit_solution(12638709530129465537)
XLA Ops:
  0.0 0.7 reshape.47
  0.7 0.1 copy.9
  0.8 0.1 reshape.56.expert_ref
  0.9 0.0 copy-start
  0.9 1.4 copy-done
  2.3 0.0 copy-start.1
  2.3 1.1 copy-done.1
  3.4 0.0 copy-start.2
  3.5 0.9 copy-done.2
  4.4 0.0 copy-start.3
  4.4 0.7 copy-done.3
  5.1 0.0 copy-start.4
  5.1 0.7 copy-done.4
  5.8 128.4 %dispatch.1 = (bf16[8,160,2048]{2,1,0:T(8,128)(2,1)S(1)}, f32[8,2,8,128]{3,2,1,0:T(8,128)S(1)}, bf16[2,2,192,2048]{3,2,1,0:T(8,128)(2,1)S(1)}, bf16[2,192,2048]{2,1,0:T(8,128)(2,1)S(1)}) custom-call(bf16[64,2048]{1,0:T(8,128)(2,1)S(1)} %copy-done.2, s32[8,64]{1,0:T(8,128)S(1)} %bitcast.26, f32[8,64]{1,0:T(8,128)S(1)} %bitcast.27, ...), custom_call_target="tpu_custom_call" | custom-call | tf_op jit(solution)/shard_map/dispatch/pallas_call | solution.py:272
  134.2 4.3 %fusion.14 = f32[1280,768]{1,0:T(8,128)S(1)} fusion(bf16[1280,2048]{1,0:T(8,128)(2,1)S(1)} %bitcast.28, bf16[768,2048]{1,0:T(8,128)(2,1)S(1)} %bitcast.29), kind=kOutput, calls=%fused_computation.22 | convolution fusion | flops 4026531840 | bytes 12320768 | tf_op jit(solution)/shard_map/dot_general | solution.py:430
  138.5 4.7 %convolution_convert_fusion = bf16[1280,2048]{1,0:T(8,128)(2,1)} fusion(bf16[384,2048]{1,0:T(8,128)(2,1)S(1)} %bitcast.30, f32[1280,768]{1,0:T(8,128)S(1)} %fusion.14), kind=kOutput, calls=%fused_computation | convolution fusion | flops 2018836480 | bytes 10747904 | tf_op jit(solution)/shard_map/dot_general | solution.py:437
  143.3 59.2 %xy_back.1 = bf16[8,160,2048]{2,1,0:T(8,128)(2,1)} custom-call(bf16[8,160,2048]{2,1,0:T(8,128)(2,1)} %bitcast.33), custom_call_target="tpu_custom_call" | custom-call | tf_op jit(solution)/shard_map/xy_back/pallas_call | solution.py:336
  202.5 0.1 convert_element_type.26
  202.6 0.0 slice-start
  202.6 0.1 squeeze.4
  202.7 0.0 slice-start.1
  202.7 5.0 %fusion.2 = f32[512,2048,1]{1,0,2:T(8,128)S(1)} fusion(bf16[8,160,2048]{2,1,0:T(8,128)(2,1)} %xy_back.1, bf16[8,512]{1,0:T(8,128)(2,1)S(1)} %get-tuple-element.16, s32[8,512]{1,0:T(8,128)S(1)} %convert_element_type.26), kind=kOutput, calls=%fused_computation.8 | convolution fusion | flops 2685665280 | bytes 9461760 | tf_op jit(solution)/shard_map/dot_general | solution.py:450
  207.7 0.0 slice-done
  207.7 0.0 slice-done.1
  207.7 3.1 %fusion = bf16[512,2048]{1,0:T(8,128)(2,1)S(1)} fusion(f32[512,2048,1]{1,0,2:T(8,128)S(1)} %fusion.2, bf16[8,160,2048]{2,1,0:T(8,128)(2,1)S(1)} %bitcast.32, bf16[8,512]{1,0:T(8,128)(2,1)S(1)} %get-tuple-element.15, s32[8,512]{1,0:T(8,128)S(1)} %convert_element_type.26), kind=kOutput, calls=%fused_computation.2 | convolution fusion | flops 2687762432 | bytes 11558912 | tf_op jit(solution)/shard_map/dot_general | solution.py:450
  210.9 40.2 %z_reduce.1 = bf16[64,2048]{1,0:T(8,128)(2,1)S(1)} custom-call(bf16[8,64,2048]{2,1,0:T(8,128)(2,1)S(1)} %bitcast.25), custom_call_target="tpu_custom_call" | custom-call | tf_op jit(solution)/shard_map/z_reduce/pallas_call | solution.py:405
  251.1 0.7 copy.14
  (6 shorter events, 0.0 us)
Async XLA Ops:
  0.9 1.4 copy-start
  2.3 1.1 copy-start.1
  3.4 0.9 copy-start.2
  4.4 0.7 copy-start.3
  5.1 0.7 copy-start.4
  202.6 5.1 %slice-start = ((s8[5242880]{0:T(1024)(128)(4,1)}), s8[1048576]{0:T(1024)(128)(4,1)S(1)}, s32[]{:S(2)}) async-start(s8[5242880]{0:T(1024)(128)(4,1)} %bitcast.31), calls=%async_computation | async-start | bytes 2097152
  202.7 5.0 %slice-start.1 = ((s8[5242880]{0:T(1024)(128)(4,1)}), s8[4194304]{0:T(1024)(128)(4,1)S(1)}, s32[]{:S(2)}) async-start(s8[5242880]{0:T(1024)(128)(4,1)} %bitcast.31), calls=%async_computation.1 | async-start | bytes 8388608

commit v3 on v2

--- a/solution.py
+++ b/solution.py
@@ -311,149 +311,198 @@
     )(tokens, ids, gates, expert, w_in, w_out)
 
 
-def back_kernel(send_ref, recv_ref, relay, local_sem, send_sem, recv_sem):
-    y, x, _ = columns()
-    mine = column_at(y, x)
-    signal_all(xy_peers())
-    own = pltpu.make_async_copy(send_ref.at[mine], recv_ref.at[mine], local_sem.at[0])
-    cols = pl.ds(0, send_ref.shape[2])
-    relays, forwards, direct = xy_copies(send_ref, recv_ref, relay, cols, send_sem, recv_sem)
-    for sent in relays + direct:
-        sent.start()
-    own.start()
-    for came, sent in zip(relays, forwards):
-        came.wait_recv()
-        sent.start()
-    for sent in direct + forwards:
-        sent.wait_recv()
-    for sent in relays + forwards + direct:
-        sent.wait_send()
-    own.wait()
-
-
-def xy_back(send):
-    _, slots, width = send.shape
-    return pl.pallas_call(
-        back_kernel,
-        out_shape=jax.ShapeDtypeStruct(send.shape, send.dtype),
-        in_specs=[pl.BlockSpec(memory_space=pl.ANY)],
-        out_specs=pl.BlockSpec(memory_space=pl.ANY),
-        scratch_shapes=[
-            pltpu.VMEM((2, Y, slots // 2, width), send.dtype),
-            pltpu.SemaphoreType.DMA((1,)),
-            pltpu.SemaphoreType.DMA((XY_COPIES,)),
-            pltpu.SemaphoreType.DMA((XY_COPIES,)),
-        ],
-        compiler_params=pltpu.CompilerParams(collective_id=2, has_side_effects=True),
-        name="xy_back",
-    )(send)
-
-
-def reduce_kernel(part_ref, out_ref, come, go, send_sem, recv_sem):
+def back_kernel(
+    hidden_ref, wout_ref, meta_ref, out_ref,
+    send, back, relay, mix, part, come, go, zs_sem, zr_sem, xs_sem, xr_sem,
+):
     base, z = z_place()
     m = z // 2
     ends = neighbours()
-    half = out_ref.shape[0] // 2
-    signal_all(ends)
+    rows, width = out_ref.shape
+    slots = send.shape[1]
+    size = width // CHUNKS
+    half = rows // 2
     last = RING // 2 - 1
-
-    def copy(way, step, chunk):
-        rows = pl.ds(chunk * half, half)
-        return pltpu.make_async_remote_copy(
-            src_ref=go.at[way, step, rows],
-            dst_ref=come.at[way, step, rows],
-            send_sem=send_sem.at[way, step, chunk],
-            recv_sem=recv_sem.at[way, step, chunk],
-            device_id={"ep": ends[way]},
-            device_id_type=MESH,
-        )
-
-    started, unread = [], {}
-    for step in range(last + 1):
-        for chunk in (0, 1):
-            for way in (0, 1):
-                if step == 0 and way != chunk:
-                    continue
-                ahead = RING // 2 - step
-                target = (m + (ahead if way == 0 else RING - ahead)) % RING
-                rows = pl.ds(chunk * half, half)
-                value = part_ref[target, rows]
-                earlier = unread.pop((way, step - 1, chunk), None)
-                if earlier is not None:
-                    earlier.wait_recv()
-                    value = (
-                        value.astype(jnp.float32) + come[way, step - 1, rows].astype(jnp.float32)
+    y, x, _ = columns()
+    mine = column_at(y, x)
+    signal_all(list(ends) + xy_peers())
+    exchanges, started, z_sent = [], [], {}
+
+    def span(chunk):
+        return pl.ds(chunk * size, size)
+
+    def produce(chunk):
+        cols = span(chunk)
+
+        @pl.loop(0, COLS)
+        def _(column):
+            send[column, :, cols] = jnp.dot(
+                hidden_ref[column], wout_ref[:, cols], preferred_element_type=jnp.float32
+            ).astype(jnp.bfloat16)
+
+        copies = xy_copies(send, back, relay, cols, xs_sem.at[chunk], xr_sem.at[chunk])
+        for sent in copies[0] + copies[2]:
+            sent.start()
+        exchanges.append(copies)
+        back[mine, :, cols] = send[mine, :, cols]
+
+    def forward(chunk):
+        relays, forwards, _ = exchanges[chunk]
+        for came, sent in zip(relays, forwards):
+            came.wait_recv()
+            sent.start()
+
+    def build_mix():
+        for pair in range(RING // 2):
+            left = lax.broadcasted_iota(jnp.int32, (COLS, 2 * rows), 1) < rows
+            slot = jnp.where(left, meta_ref[2 * pair, 0], meta_ref[2 * pair + 1, 0])
+            gate = jnp.where(left, meta_ref[2 * pair, 1], meta_ref[2 * pair + 1, 1])
+            first = lax.broadcasted_iota(jnp.int32, slot.shape, 0) * slots
+            slot = jnp.where(slot < 0.0, -1.0, slot + first.astype(jnp.float32)).T
+            gate = gate.T
+            high = gate.astype(jnp.bfloat16).astype(jnp.float32)
+            low = gate - high
+            for lane in range(0, COLS * slots, 128):
+                place = lax.broadcasted_iota(jnp.int32, (2 * rows, 128), 1) + lane
+                place = place.astype(jnp.float32)
+                tops = jnp.zeros(place.shape, jnp.float32)
+                rest = jnp.zeros(place.shape, jnp.float32)
+                for column in range(lane // slots, (lane + 127) // slots + 1):
+                    hit = place == slot[:, column : column + 1]
+                    tops += jnp.where(hit, high[:, column : column + 1], 0.0)
+                    rest += jnp.where(hit, low[:, column : column + 1], 0.0)
+                here = pl.ds(pair * 2 * rows, 2 * rows), pl.ds(lane, 128)
+                mix[0, here[0], here[1]] = tops.astype(jnp.bfloat16)
+                mix[1, here[0], here[1]] = rest.astype(jnp.bfloat16)
+
+    def merge(chunk):
+        cols = span(chunk)
+        _, forwards, direct = exchanges[chunk]
+        for sent in direct + forwards:
+            sent.wait_recv()
+        tile = 256
+
+        @pl.loop(0, RING * rows // tile)
+        def _(step):
+            here = pl.ds(pl.multiple_of(step * tile, tile), tile)
+            values = back[:, :, cols].reshape(COLS * slots, size)
+            part[here, cols] = jnp.dot(
+                mix[0, here], values, preferred_element_type=jnp.float32
+            ) + jnp.dot(mix[1, here], values, preferred_element_type=jnp.float32)
+
+    def reduce_step(chunk, step):
+        cols = span(chunk)
+        for way in (0, 1):
+            ahead = RING // 2 - step
+            target = (m + (ahead if way == 0 else RING - ahead)) % RING
+            count = half if step == 0 else rows
+            first = way * half if step == 0 else 0
+            value = part[pl.ds(target * rows + first, count), cols]
+            local = pl.ds(first, count)
+            if step == 0:
+                go[way, step, local, cols] = value.astype(jnp.bfloat16)
+            else:
+                z_sent[way, step - 1, chunk].wait_recv()
+                if step == 1:
+                    touched = pl.ds(way * half, half)
+                    other = (1 - way) * half
+                    arrived = come[way, 0, touched, cols].astype(jnp.float32)
+                    go[way, 1, touched, cols] = (
+                        value[way * half : way * half + half] + arrived
                     ).astype(jnp.bfloat16)
-                go[way, step, rows] = value
-                sent = copy(way, step, chunk)
-                sent.start()
-                started.append(sent)
-                unread[way, step, chunk] = sent
-    for chunk in (0, 1):
-        rows = pl.ds(chunk * half, half)
-        total = part_ref[m, rows].astype(jnp.float32)
+                    go[way, 1, pl.ds(other, half), cols] = value[other : other + half].astype(
+                        jnp.bfloat16
+                    )
+                else:
+                    arrived = come[way, step - 1, :, cols].astype(jnp.float32)
+                    go[way, step, :, cols] = (value + arrived).astype(jnp.bfloat16)
+            sent = pltpu.make_async_remote_copy(
+                src_ref=go.at[way, step, local, cols],
+                dst_ref=come.at[way, step, local, cols],
+                send_sem=zs_sem.at[way, step, chunk],
+                recv_sem=zr_sem.at[way, step, chunk],
+                device_id={"ep": ends[way]},
+                device_id_type=MESH,
+            )
+            sent.start()
+            started.append(sent)
+            z_sent[way, step, chunk] = sent
+
+    def finish(chunk):
+        cols = span(chunk)
+        total = part[pl.ds(m * rows, rows), cols]
         for way in (0, 1):
-            unread.pop((way, last, chunk)).wait_recv()
-            total += come[way, last, rows].astype(jnp.float32)
-        out_ref[rows] = total.astype(jnp.bfloat16)
+            z_sent[way, last, chunk].wait_recv()
+            total += come[way, last, :, cols].astype(jnp.float32)
+        out_ref[:, cols] = total.astype(jnp.bfloat16)
+
+    produce(0)
+    build_mix()
+    forward(0)
+    produce(1)
+    for chunk in range(CHUNKS):
+        merge(chunk)
+        reduce_step(chunk, 0)
+        if chunk:
+            finish(chunk - 1)
+        reduce_step(chunk, 1)
+        if chunk + 1 < CHUNKS:
+            forward(chunk + 1)
+        if chunk + 2 < CHUNKS:
+            produce(chunk + 2)
+        reduce_step(chunk, 2)
+        reduce_step(chunk, 3)
+    finish(CHUNKS - 1)
+    for relays, forwards, direct in exchanges:
+        for sent in relays + forwards + direct:
+            sent.wait_send()
     for sent in started:
         sent.wait_send()
 
 
-def z_reduce(part):
-    _, rows, width = part.shape
+def combine(hidden, w_out, meta):
+    _, slots, ff = hidden.shape
+    width = w_out.shape[1]
+    rows = meta.shape[3] // 2
+    dma = pltpu.SemaphoreType.DMA
     return pl.pallas_call(
-        reduce_kernel,
-        out_shape=jax.ShapeDtypeStruct((rows, width), part.dtype),
-        in_specs=[pl.BlockSpec(memory_space=pltpu.VMEM)],
+        back_kernel,
+        out_shape=jax.ShapeDtypeStruct((rows, width), w_out.dtype),
+        in_specs=[pl.BlockSpec(memory_space=pltpu.VMEM)] * 3,
         out_specs=pl.BlockSpec(memory_space=pltpu.VMEM),
         scratch_shapes=[
-            pltpu.VMEM((2, RING // 2, rows, width), part.dtype),
-            pltpu.VMEM((2, RING // 2, rows, width), part.dtype),
-            pltpu.SemaphoreType.DMA((2, RING // 2, 2)),
-            pltpu.SemaphoreType.DMA((2, RING // 2, 2)),
+            pltpu.VMEM((COLS, slots, width), w_out.dtype),
+            pltpu.VMEM((COLS, slots, width), w_out.dtype),
+            pltpu.VMEM((2, Y, slots // 2, width), w_out.dtype),
+            pltpu.VMEM((2, RING * rows, COLS * slots), w_out.dtype),
+            pltpu.VMEM((RING * rows, width), jnp.float32),
+            pltpu.VMEM((2, RING // 2, rows, width), w_out.dtype),
+            pltpu.VMEM((2, RING // 2, rows, width), w_out.dtype),
+            dma((2, RING // 2, CHUNKS)),
+            dma((2, RING // 2, CHUNKS)),
+            dma((CHUNKS, XY_COPIES)),
+            dma((CHUNKS, XY_COPIES)),
         ],
         compiler_params=pltpu.CompilerParams(
-            collective_id=3, has_side_effects=True, vmem_limit_bytes=32 << 20
+            collective_id=2, has_side_effects=True, vmem_limit_bytes=48 << 20
         ),
-        name="z_reduce",
-    )(part)
+        name="combine",
+    )(hidden, w_out, meta)
 
 
 def local(tokens, gates, expert_ids, slot_expert, w_in, w_out):
-    rows, width = tokens.shape
     expert = slot_expert.reshape(COLS, Z // GROUP).T.reshape(-1, 1)
     recv, meta, win2, wout2 = dispatch(tokens, expert_ids.T, gates.T, expert, w_in, w_out)
-    slots = RING * CAPE
-    recv = recv.reshape(COLS * slots, width)
+    _, slots, width = recv.shape
     ff = win2.shape[1] * win2.shape[2]
     both = lax.dot_general(
-        recv,
+        recv.reshape(COLS * slots, width),
         win2.reshape(2 * ff, width),
         (((1,), (1,)), ((), ())),
         preferred_element_type=jnp.float32,
     )
     hidden = (jax.nn.silu(both[:, :ff]) * both[:, ff:]).astype(jnp.bfloat16)
-    produced = jnp.dot(
-        hidden, wout2.reshape(ff, width), preferred_element_type=jnp.float32
-    ).astype(jnp.bfloat16)
-    back = xy_back(produced.reshape(COLS, slots, width)).reshape(COLS * slots, width)
-    meta = meta[..., :rows].transpose(1, 2, 0, 3).reshape(2, COLS, RING * rows)
-    slot, gate = meta[0].astype(jnp.int32), meta[1]
-    hit = jnp.arange(slots, dtype=jnp.int32)[None, :, None] == slot[:, None, :]
-    high = lax.reduce_precision(gate, 8, 7)
-    low = gate - high
-    zero = jnp.zeros((), jnp.float32)
-    part = jnp.zeros((RING * rows, width), jnp.float32)
-    for piece in (high, low):
-        mix = jnp.where(hit, piece[:, None, :], zero).astype(jnp.bfloat16)
-        part += lax.dot_general(
-            mix.reshape(COLS * slots, RING * rows),
-            back,
-            (((0,), (0,)), ((), ())),
-            preferred_element_type=jnp.float32,
-        )
-    return z_reduce(part.astype(jnp.bfloat16).reshape(RING, rows, width))
+    return combine(hidden.reshape(COLS, slots, ff), wout2.reshape(ff, width), meta)
 
 
 def solution(mesh):

time: 252 us -> 241 us (0.956)
  the two profiles are of different devices: /device:TPU:10 before, /device:TPU:50 now
where the time goes in v3:
time: 241 us
  Pallas kernels  230 us (95%)
  local copies, waits for them, and re-layouts  6.47 us (3%)
  matrix products  4.36 us (2%)
    pallas_call x1, Pallas kernels, dispatch(): pl.pallas_call(out_kernel, out_shape=(jax.ShapeDtypeStruct((COLS, slots,...  126 us
    pallas_call x1, Pallas kernels, combine(): pl.pallas_call(back_kernel, out_shape=jax.ShapeDtypeStruct((rows, width),...  103 us
    unnamed x11, local copies, waits for them, and re-layouts  5.58 us

profile of v3, /device:TPU:50, one launch (start us, length us, event | category | flops | bytes accessed | tf_op | source)
XLA Modules:
  0.0 241.1 jit_solution(12663875873278501135)
XLA Ops:
  0.0 0.7 reshape.18
  0.7 0.1 copy.9
  0.8 0.1 reshape.24.expert_ref
  0.9 0.0 copy-start
  0.9 1.4 copy-done
  2.3 0.0 copy-start.1
  2.3 1.1 copy-done.1
  3.4 0.0 copy-start.2
  3.5 0.9 copy-done.2
  4.4 0.0 copy-start.3
  4.4 0.7 copy-done.3
  5.1 0.0 copy-start.4
  5.1 0.7 copy-done.4
  5.8 126.3 %dispatch.1 = (bf16[8,160,2048]{2,1,0:T(8,128)(2,1)S(1)}, f32[8,2,8,128]{3,2,1,0:T(8,128)S(1)}, bf16[2,2,192,2048]{3,2,1,0:T(8,128)(2,1)S(1)}, bf16[2,192,2048]{2,1,0:T(8,128)(2,1)S(1)}) custom-call(bf16[64,2048]{1,0:T(8,128)(2,1)S(1)} %copy-done.2, s32[8,64]{1,0:T(8,128)S(1)} %bitcast.11, f32[8,64]{1,0:T(8,128)S(1)} %bitcast.12, ...), custom_call_target="tpu_custom_call" | custom-call | tf_op jit(solution)/shard_map/dispatch/pallas_call | solution.py:272
  132.1 4.4 %fusion.1 = f32[1280,768]{1,0:T(8,128)S(1)} fusion(bf16[1280,2048]{1,0:T(8,128)(2,1)S(1)} %bitcast.13, bf16[768,2048]{1,0:T(8,128)(2,1)S(1)} %bitcast.14), kind=kOutput, calls=%fused_computation.2 | convolution fusion | flops 4026531840 | bytes 12320768 | tf_op jit(solution)/shard_map/dot_general | solution.py:498
  136.5 0.6 fusion
  137.0 103.3 %combine.1 = bf16[64,2048]{1,0:T(8,128)(2,1)S(1)} custom-call(bf16[8,160,384]{2,1,0:T(8,128)(2,1)S(1)} %bitcast.9, bf16[384,2048]{1,0:T(8,128)(2,1)S(1)} %bitcast.10, f32[8,2,8,128]{3,2,1,0:T(8,128)S(1)} %get-tuple-element.12.meta_ref), custom_call_target="tpu_custom_call" | custom-call | tf_op jit(solution)/shard_map/combine/pallas_call | solution.py:468
  240.4 0.7 copy.12
Async XLA Ops:
  0.9 1.4 copy-start
  2.3 1.1 copy-start.1
  3.4 0.9 copy-start.2
  4.4 0.7 copy-start.3
  5.1 0.7 copy-start.4

commit v4 on v3

v4 whole, which is shorter than its diff:
```python
import jax
import jax.numpy as jnp
from jax import lax
from jax.experimental import pallas as pl
from jax.experimental.pallas import tpu as pltpu
from jax.sharding import PartitionSpec as P

MESH = pl.DeviceIdType.MESH
GROUP = 4
CAPE = 20
Z = 16
X = 4
Y = 2
RING = Z // 2
COLS = X * Y
CHUNKS = 4
PIECES = 4
EARLY = (0, 1, 1, 1)


def z_place():
    me = lax.axis_index("ep")
    z = me % Z
    return me - z, z


def neighbours():
    base, z = z_place()
    return base + (z + 2) % Z, base + (z + Z - 2) % Z


def signal_all(devices):
    barrier = pltpu.get_barrier_semaphore()
    for device in devices:
        pl.semaphore_signal(barrier, inc=1, device_id={"ep": device}, device_id_type=MESH)
    pl.semaphore_wait(barrier, len(devices))


def columns():
    me = lax.axis_index("ep")
    return me // (X * Z), me // Z % X, me % Z


def column_at(y, x):
    return y % Y * X + x % X


def xy_peers():
    y, x, z = columns()
    return [
        column_at(y + ky, x + kx) * Z + z for ky in range(Y) for kx in range(X) if kx or ky
    ]


def xy_copies(send_ref, recv_ref, relay_ref, send_sem, recv_sem):
    y, x, z = columns()
    mine = column_at(y, x)
    half = send_ref.shape[1] // 2

    def remote(k, src, dst, column):
        return pltpu.make_async_remote_copy(
            src_ref=src,
            dst_ref=dst,
            send_sem=send_sem.at[k],
            recv_sem=recv_sem.at[k],
            device_id={"ep": column * Z + z},
            device_id_type=MESH,
        )

    relays, forwards, direct = [], [], []
    for way, step in ((0, 1), (1, X - 1)):
        rows = pl.ds(way * half, half)
        for ky in range(Y):
            k = 2 * way + ky
            slot = relay_ref.at[k]
            relays.append(
                remote(k, send_ref.at[column_at(y + ky, x + 2), rows], slot, column_at(y, x + step))
            )
            forwards.append(
                remote(
                    4 + k,
                    slot,
                    recv_ref.at[column_at(y, x + X - step), rows],
                    column_at(y + ky, x + step),
                )
            )
    for k, (ky, kx) in enumerate(((1, 1), (1, 3), (1, 0), (0, 1), (0, 3))):
        other = column_at(y + ky, x + kx)
        direct.append(remote(8 + k, send_ref.at[other], recv_ref.at[mine], other))
    return relays, forwards, direct


XY_COPIES = 13


def layer_kernel(
    tok_ref, ids_ref, gates_ref, expert_ref, win_ref, wout_ref, out_ref,
    held, table, meta, pick, send, recv, relay, win2, wout2, act, hidden,
    back, relay2, mix, part, come, go,
    own_sem, zs_sem, zr_sem, ms_sem, mr_sem, xs_sem, xr_sem, ws_sem, wr_sem, wl_sem,
    rs_sem, rr_sem, bs_sem, br_sem,
):
    base, z = z_place()
    m, member = z // 2, z % 2
    ends = neighbours()
    rows, width = tok_ref.shape
    slots = pick.shape[1]
    size = width // CHUNKS
    half = rows // 2
    last = RING // 2 - 1
    y, x, _ = columns()
    mine = column_at(y, x)
    partner = mine * Z + z + 1 - 2 * member

    def span(chunk):
        return pl.ds(chunk * size, size)

    own = []
    for chunk in range(CHUNKS):
        own.append(
            pltpu.make_async_copy(
                tok_ref.at[:, span(chunk)], held.at[chunk, pl.ds(m * rows, rows)], own_sem.at[chunk]
            )
        )
        own[-1].start()
    ring = [base + (z + 2 * k) % Z for k in range(1, RING)]
    signal_all(ring + [partner] + xy_peers())

    z_sent, started = {}, []

    def z_go(chunk, step):
        if step == 0:
            own[chunk].wait()
        for way in (0, 1):
            if step:
                z_sent[way, step - 1, chunk].wait_recv()
            owner = (m + (RING - step if way == 0 else step)) % RING
            count = half if step == last else rows
            first = way * half if step == last else 0
            there = held.at[chunk, pl.ds(owner * rows + first, count)]
            sent = pltpu.make_async_remote_copy(
                src_ref=there,
                dst_ref=there,
                send_sem=zs_sem.at[way, step, chunk],
                recv_sem=zr_sem.at[way, step, chunk],
                device_id={"ep": ends[way]},
                device_id_type=MESH,
            )
            sent.start()
            z_sent[way, step, chunk] = sent
            started.append(sent)

    queue = sorted(
        ((chunk, step) for chunk in range(CHUNKS) for step in range(last + 1)),
        key=lambda place: (2 * place[0] + place[1], place[0]),
    )
    z_go(*queue.pop(0))

    chosen = jnp.zeros((Z // GROUP * COLS, rows), jnp.float32)
    gate = jnp.zeros((Z // GROUP * COLS, rows), jnp.float32)
    for k in range(ids_ref.shape[0]):
        same = ids_ref[pl.ds(k, 1), :] == expert_ref[...]
        chosen += jnp.where(same, 1.0, 0.0)
        gate += jnp.where(same, gates_ref[pl.ds(k, 1), :], 0.0)
    earlier = lax.broadcasted_iota(jnp.int32, (rows, rows), 0) < lax.broadcasted_iota(
        jnp.int32, (rows, rows), 1
    )
    rank = jnp.dot(
        chosen.astype(jnp.bfloat16),
        jnp.where(earlier, 1.0, 0.0).astype(jnp.bfloat16),
        preferred_element_type=jnp.float32,
    )
    slot = jnp.where(chosen > 0.5, rank + (m * CAPE).astype(jnp.float32), -1.0)
    table[:, 0] = jnp.concatenate([slot, slot], axis=1).reshape(Z // GROUP, COLS, 2 * rows)
    table[:, 1] = jnp.concatenate([gate, gate], axis=1).reshape(Z // GROUP, COLS, 2 * rows)
    metas = []
    for k in range(1, RING):
        other = (m + k) % RING
        metas.append(
            pltpu.make_async_remote_copy(
                src_ref=table.at[other // 2],
                dst_ref=meta.at[m],
                send_sem=ms_sem.at[k - 1],
                recv_sem=mr_sem.at[k - 1],
                device_id={"ep": base + (z + 2 * k) % Z},
                device_id_type=MESH,
            )
        )
        metas[-1].start()
    meta[m] = table[m // 2]

    def paired(pair, kind):
        left = lax.broadcasted_iota(jnp.int32, (COLS, 2 * rows), 1) < rows
        return jnp.where(left, meta[2 * pair, kind], meta[2 * pair + 1, kind])

    def build_pick():
        for pair in range(RING // 2):
            both = paired(pair, 0)
            place = lax.broadcasted_iota(jnp.int32, (slots, 2 * rows), 0).astype(jnp.float32)
            for column in range(COLS):
                hit = place == jnp.broadcast_to(both[column : column + 1], place.shape)
                pick[column, :, pl.ds(pair * 2 * rows, 2 * rows)] = jnp.where(
                    hit, 1.0, 0.0
                ).astype(jnp.bfloat16)

    def build_mix():
        for pair in range(RING // 2):
            slot, gate = paired(pair, 0), paired(pair, 1)
            first = lax.broadcasted_iota(jnp.int32, slot.shape, 0) * slots
            slot = jnp.where(slot < 0.0, -1.0, slot + first.astype(jnp.float32)).T
            gate = gate.T
            high = gate.astype(jnp.bfloat16).astype(jnp.float32)
            low = gate - high
            for lane in range(0, COLS * slots, 128):
                place = lax.broadcasted_iota(jnp.int32, (2 * rows, 128), 1) + lane
                place = place.astype(jnp.float32)
                tops = jnp.zeros(place.shape, jnp.float32)
                rest = jnp.zeros(place.shape, jnp.float32)
                for column in range(lane // slots, (lane + 127) // slots + 1):
                    hit = place == slot[:, column : column + 1]
                    tops += jnp.where(hit, high[:, column : column + 1], 0.0)
                    rest += jnp.where(hit, low[:, column : column + 1], 0.0)
                here = pl.ds(pair * 2 * rows, 2 * rows), pl.ds(lane, 128)
                mix[0, here[0], here[1]] = tops.astype(jnp.bfloat16)
                mix[1, here[0], here[1]] = rest.astype(jnp.bfloat16)

    ff = win_ref.shape[2]
    count = ff // PIECES
    pieces = []
    for piece in range(PIECES):
        here = pl.ds(piece * count, count)
        for side in (0, 1):
            there = pl.ds((2 * side + member) * ff + piece * count, count)
            pieces.append((win_ref.at[0, side, here], win2.at[there]))
    for piece in range(PIECES):
        here = pl.ds(piece * count, count)
        there = pl.ds(member * ff + piece * count, count)
        pieces.append((wout_ref.at[0, here], wout2.at[there]))
    weights, kept = [], []

    def weight_go(src, dst):
        k = len(weights)
        weights.append(
            pltpu.make_async_remote_copy(
                src_ref=src,
                dst_ref=dst,
                send_sem=ws_sem.at[k],
                recv_sem=wr_sem.at[k],
                device_id={"ep": partner},
                device_id_type=MESH,
            )
        )
        weights[-1].start()
        kept.append(pltpu.make_async_copy(src, dst, wl_sem.at[k]))
        kept[-1].start()

    def forward(copies):
        relays, forwards, _ = copies
        for came, sent in zip(relays, forwards):
            came.wait_recv()
            sent.start()

    exchanges = []
    for chunk in range(CHUNKS):
        while queue and 2 * queue[0][0] + queue[0][1] <= 2 * chunk + last:
            z_go(*queue.pop(0))
        for _ in range(EARLY[chunk] if queue else len(pieces)):
            weight_go(*pieces.pop(0))
        if chunk == 0:
            for sent in metas:
                sent.wait_recv()
            build_pick()
        else:
            forward(exchanges[-1])
        for way in (0, 1):
            z_sent[way, last, chunk].wait_recv()

        @pl.loop(0, COLS)
        def _(column):
            send[chunk, column] = jnp.dot(
                pick[column], held[chunk], preferred_element_type=jnp.float32
            ).astype(jnp.bfloat16)

        copies = xy_copies(
            send.at[chunk], recv.at[chunk], relay.at[chunk], xs_sem.at[chunk], xr_sem.at[chunk]
        )
        for sent in copies[0] + copies[2]:
            sent.start()
        exchanges.append(copies)
        recv[chunk, mine] = send[chunk, mine]
    build_mix()
    forward(exchanges[-1])

    tile = COLS * slots // 4
    group = COLS // 4
    for k in range(2 * PIECES):
        weights[k].wait_recv()
        kept[k].wait()
    for chunk in range(CHUNKS):
        _, forwards, direct = exchanges[chunk]
        for sent in direct + forwards:
            sent.wait_recv()

        @pl.loop(0, 4)
        def _(step):
            here = pl.ds(pl.multiple_of(step * tile, tile), tile)
            term = lax.dot_general(
                recv[chunk, pl.ds(step * group, group)].reshape(tile, size),
                win2[:, span(chunk)],
                (((1,), (1,)), ((), ())),
                preferred_element_type=jnp.float32,
            )
            if chunk:
                term += act[here]
            if chunk < CHUNKS - 1:
                act[here] = term
            else:
                side = wout2.shape[0]
                value = term[:, :side]
                value = value / (1.0 + jnp.exp(-value)) * term[:, side:]
                hidden[here] = value.astype(jnp.bfloat16)

    for relays, forwards, direct in exchanges:
        for sent in relays + forwards + direct:
            sent.wait_send()
    for k in range(2 * PIECES, 3 * PIECES):
        weights[k].wait_recv()
        kept[k].wait()

    exchanges, r_sent = [], {}

    def produce(chunk):
        @pl.loop(0, 4)
        def _(step):
            here = pl.ds(pl.multiple_of(step * tile, tile), tile)
            send[chunk, pl.ds(step * group, group)] = (
                jnp.dot(hidden[here], wout2[:, span(chunk)], preferred_element_type=jnp.float32)
                .astype(jnp.bfloat16)
                .reshape(group, slots, size)
            )

        copies = xy_copies(
            send.at[chunk], back.at[chunk], relay2.at[chunk], bs_sem.at[chunk], br_sem.at[chunk]
        )
        for sent in copies[0] + copies[2]:
            sent.start()
        exchanges.append(copies)
        back[chunk, mine] = send[chunk, mine]

    def merge(chunk):
        _, forwards, direct = exchanges[chunk]
        for sent in direct + forwards:
            sent.wait_recv()
        block = 256

        @pl.loop(0, RING * rows // block)
        def _(step):
            here = pl.ds(pl.multiple_of(step * block, block), block)
            values = back[chunk].reshape(COLS * slots, size)
            part[chunk, here] = jnp.dot(
                mix[0, here], values, preferred_element_type=jnp.float32
            ) + jnp.dot(mix[1, here], values, preferred_element_type=jnp.float32)

    def reduce_step(chunk, step):
        for way in (0, 1):
            ahead = RING // 2 - step
            target = (m + (ahead if way == 0 else RING - ahead)) % RING
            count = half if step == 0 else rows
            first = way * half if step == 0 else 0
            value = part[chunk, pl.ds(target * rows + first, count)]
            local = pl.ds(first, count)
            if step == 0:
                go[chunk, way, step, local] = value.astype(jnp.bfloat16)
            else:
                r_sent[way, step - 1, chunk].wait_recv()
                if step == 1:
                    touched = pl.ds(way * half, half)
                    other = (1 - way) * half
                    arrived = come[chunk, way, 0, touched].astype(jnp.float32)
                    go[chunk, way, 1, touched] = (
                        value[way * half : way * half + half] + arrived
                    ).astype(jnp.bfloat16)
                    go[chunk, way, 1, pl.ds(other, half)] = value[other : other + half].astype(
                        jnp.bfloat16
                    )
                else:
                    arrived = come[chunk, way, step - 1].astype(jnp.float32)
                    go[chunk, way, step] = (value + arrived).astype(jnp.bfloat16)
            sent = pltpu.make_async_remote_copy(
                src_ref=go.at[chunk, way, step, local],
                dst_ref=come.at[chunk, way, step, local],
                send_sem=rs_sem.at[way, step, chunk],
                recv_sem=rr_sem.at[way, step, chunk],
                device_id={"ep": ends[way]},
                device_id_type=MESH,
            )
            sent.start()
            started.append(sent)
            r_sent[way, step, chunk] = sent

    def finish(chunk):
        total = part[chunk, pl.ds(m * rows, rows)]
        for way in (0, 1):
            r_sent[way, last, chunk].wait_recv()
            total += come[chunk, way, last].astype(jnp.float32)
        out_ref[:, span(chunk)] = total.astype(jnp.bfloat16)

    produce(0)
    produce(1)
    forward(exchanges[0])
    for chunk in range(CHUNKS):
        merge(chunk)
        reduce_step(chunk, 0)
        if chunk + 1 < CHUNKS:
            forward(exchanges[chunk + 1])
        if chunk + 2 < CHUNKS:
            produce(chunk + 2)
        if chunk:
            reduce_step(chunk - 1, 3)
        reduce_step(chunk, 1)
        if chunk:
            finish(chunk - 1)
        reduce_step(chunk, 2)
    reduce_step(CHUNKS - 1, 3)
    finish(CHUNKS - 1)
    for relays, forwards, direct in exchanges:
        for sent in relays + forwards + direct:
            sent.wait_send()
    for sent in started + metas + weights:
        sent.wait_send()


def layer(tokens, ids, gates, expert, w_in, w_out):
    rows, width = tokens.shape
    _, two, ff, _ = w_in.shape
    slots = RING * CAPE
    steps = RING // 2
    size = width // CHUNKS
    kind = tokens.dtype
    dma = pltpu.SemaphoreType.DMA
    return pl.pallas_call(
        layer_kernel,
        out_shape=jax.ShapeDtypeStruct((rows, width), kind),
        in_specs=[pl.BlockSpec(memory_space=pl.ANY)]
        + [pl.BlockSpec(memory_space=pltpu.VMEM)] * 3
        + [pl.BlockSpec(memory_space=pl.ANY)] * 2,
        out_specs=pl.BlockSpec(memory_space=pltpu.VMEM),
        scratch_shapes=[
            pltpu.VMEM((CHUNKS, RING * rows, size), kind),
            pltpu.VMEM((Z // GROUP, 2, COLS, 2 * rows), jnp.float32),
            pltpu.VMEM((RING, 2, COLS, 2 * rows), jnp.float32),
            pltpu.VMEM((COLS, slots, RING * rows), kind),
            pltpu.VMEM((CHUNKS, COLS, slots, size), kind),
            pltpu.VMEM((CHUNKS, COLS, slots, size), kind),
            pltpu.VMEM((CHUNKS, 2 * Y, slots // 2, size), kind),
            pltpu.VMEM((two * 2 * ff, width), kind),
            pltpu.VMEM((2 * ff, width), kind),
            pltpu.VMEM((COLS * slots, two * 2 * ff), jnp.float32),
            pltpu.VMEM((COLS * slots, 2 * ff), kind),
            pltpu.VMEM((CHUNKS, COLS, slots, size), kind),
            pltpu.VMEM((CHUNKS, 2 * Y, slots // 2, size), kind),
            pltpu.VMEM((2, RING * rows, COLS * slots), kind),
            pltpu.VMEM((CHUNKS, RING * rows, size), jnp.float32),
            pltpu.VMEM((CHUNKS, 2, steps, rows, size), kind),
            pltpu.VMEM((CHUNKS, 2, steps, rows, size), kind),
            dma((CHUNKS,)),
            dma((2, steps, CHUNKS)),
            dma((2, steps, CHUNKS)),
            dma((RING - 1,)),
            dma((RING - 1,)),
            dma((CHUNKS, XY_COPIES)),
            dma((CHUNKS, XY_COPIES)),
            dma((3 * PIECES,)),
            dma((3 * PIECES,)),
            dma((3 * PIECES,)),
            dma((2, steps, CHUNKS)),
            dma((2, steps, CHUNKS)),
            dma((CHUNKS, XY_COPIES)),
            dma((CHUNKS, XY_COPIES)),
        ],
        compiler_params=pltpu.CompilerParams(
            collective_id=0, has_side_effects=True, vmem_limit_bytes=60 << 20
        ),
        name="layer",
    )(tokens, ids, gates, expert, w_in, w_out)


def local(tokens, gates, expert_ids, slot_expert, w_in, w_out):
    expert = slot_expert.reshape(COLS, Z // GROUP).T.reshape(-1, 1)
    return layer(tokens, expert_ids.T, gates.T, expert, w_in, w_out)


def solution(mesh):
    return jax.shard_map(
        local,
        mesh=mesh,
        in_specs=(
            P(("dp", "ep"), None),
            P(("dp", "ep"), None),
            P(("dp", "ep"), None),
            P("dp"),
            P(("dp", "ep"), None, None, None),
            P(("dp", "ep"), None, None),
        ),
        out_specs=P(("dp", "ep"), None),
        check_vma=False,
    )
```

time: 241 us -> 216 us (0.90)
  the two profiles are of different devices: /device:TPU:50 before, /device:TPU:60 now
where the time goes in v4:
time: 216 us
  Pallas kernels  213 us (99%)
  local copies, waits for them, and re-layouts  3.18 us (1%)
    pallas_call x1, Pallas kernels, layer(): pl.pallas_call(layer_kernel, out_shape=jax.ShapeDtypeStruct((rows, width)...  213 us

profile of v4, /device:TPU:60, one launch (start us, length us, event | category | flops | bytes accessed | tf_op | source)
XLA Modules:
  0.0 216.2 jit_solution(2543307252191344186)
XLA Ops:
  0.0 0.7 reshape.6
  0.7 0.1 copy.9
  0.8 0.7 reshape.8.expert_ref
  1.5 213.0 %layer.1 = bf16[64,2048]{1,0:T(8,128)(2,1)} custom-call(bf16[64,2048]{1,0:T(8,128)(2,1)} %tok_ref.1, s32[8,64]{1,0:T(8,128)} %bitcast.4, f32[8,64]{1,0:T(8,128)} %bitcast.5, s32[32,1]{1,0:T(8,128)} %reshape.8.expert_ref, bf16[1,2,192,2048]{3,2,1,0:T(8,128)(2,1)} %win_ref.1, bf16[1,192,2048]{2,1,0:T(8,128)(2,1)} %wout_ref.1), custom_call_target="tpu_custom_call" | custom-call | tf_op jit(solution)/shard_map/layer/pallas_call | solution.py:441
  214.5 1.7 copy.12

commit v5 on v4

--- a/solution.py
+++ b/solution.py
@@ -13,9 +13,10 @@
 Y = 2
 RING = Z // 2
 COLS = X * Y
-CHUNKS = 4
+WIDTHS = (512, 512, 512, 512)
+CHUNKS = len(WIDTHS)
 PIECES = 4
-EARLY = (0, 1, 1, 1)
+EARLY = (0, 2, 2, 2)
 
 
 def z_place():
@@ -94,10 +95,10 @@
 
 
 def layer_kernel(
-    tok_ref, ids_ref, gates_ref, expert_ref, win_ref, wout_ref, out_ref,
-    held, table, meta, pick, send, recv, relay, win2, wout2, act, hidden,
+    tok_ref, ids_hbm, gates_hbm, expert_ref, win_ref, wout_ref, out_ref,
+    held, ids_ref, gates_ref, table, meta, pick, send, recv, relay, win2, wout2, act, hidden,
     back, relay2, mix, part, come, go,
-    own_sem, zs_sem, zr_sem, ms_sem, mr_sem, xs_sem, xr_sem, ws_sem, wr_sem, wl_sem,
+    own_sem, small_sem, zs_sem, zr_sem, ms_sem, mr_sem, xs_sem, xr_sem, ws_sem, wr_sem, wl_sem, wo_sem,
     rs_sem, rr_sem, bs_sem, br_sem,
 ):
     base, z = z_place()
@@ -105,7 +106,6 @@
     ends = neighbours()
     rows, width = tok_ref.shape
     slots = pick.shape[1]
-    size = width // CHUNKS
     half = rows // 2
     last = RING // 2 - 1
     y, x, _ = columns()
@@ -113,16 +113,32 @@
     partner = mine * Z + z + 1 - 2 * member
 
     def span(chunk):
-        return pl.ds(chunk * size, size)
+        return pl.ds(sum(WIDTHS[:chunk]), WIDTHS[chunk])
 
     own = []
     for chunk in range(CHUNKS):
         own.append(
             pltpu.make_async_copy(
-                tok_ref.at[:, span(chunk)], held.at[chunk, pl.ds(m * rows, rows)], own_sem.at[chunk]
+                tok_ref.at[:, span(chunk)], held[chunk].at[pl.ds(m * rows, rows)], own_sem.at[chunk]
             )
         )
         own[-1].start()
+    small = [
+        pltpu.make_async_copy(ids_hbm, ids_ref, small_sem.at[0]),
+        pltpu.make_async_copy(gates_hbm, gates_ref, small_sem.at[1]),
+    ]
+    for piece in small:
+        piece.start()
+    ff = win_ref.shape[2]
+    mine_out = pl.ds(member * ff, ff)
+    own_out = []
+    for chunk in range(CHUNKS):
+        own_out.append(
+            pltpu.make_async_copy(
+                wout_ref.at[0, :, span(chunk)], wout2[chunk].at[mine_out], wo_sem.at[chunk]
+            )
+        )
+        own_out[-1].start()
     ring = [base + (z + 2 * k) % Z for k in range(1, RING)]
     signal_all(ring + [partner] + xy_peers())
 
@@ -137,7 +153,7 @@
             owner = (m + (RING - step if way == 0 else step)) % RING
             count = half if step == last else rows
             first = way * half if step == last else 0
-            there = held.at[chunk, pl.ds(owner * rows + first, count)]
+            there = held[chunk].at[pl.ds(owner * rows + first, count)]
             sent = pltpu.make_async_remote_copy(
                 src_ref=there,
                 dst_ref=there,
@@ -156,10 +172,20 @@
     )
     z_go(*queue.pop(0))
 
-    chosen = jnp.zeros((Z // GROUP * COLS, rows), jnp.float32)
-    gate = jnp.zeros((Z // GROUP * COLS, rows), jnp.float32)
+    for piece in small:
+        piece.wait()
+    groups = Z // GROUP * COLS
+    line = lax.broadcasted_iota(jnp.int32, (groups, groups), 0)
+    wanted = lax.broadcasted_iota(jnp.int32, (groups, groups), 1) == (
+        line % COLS * (Z // GROUP) + line // COLS
+    )
+    expert = jnp.sum(
+        jnp.where(wanted, expert_ref[...].astype(jnp.float32), 0.0), axis=1, keepdims=True
+    ).astype(jnp.int32)
+    chosen = jnp.zeros((groups, rows), jnp.float32)
+    gate = jnp.zeros((groups, rows), jnp.float32)
     for k in range(ids_ref.shape[0]):
-        same = ids_ref[pl.ds(k, 1), :] == expert_ref[...]
+        same = ids_ref[pl.ds(k, 1), :] == expert
         chosen += jnp.where(same, 1.0, 0.0)
         gate += jnp.where(same, gates_ref[pl.ds(k, 1), :], 0.0)
     earlier = lax.broadcasted_iota(jnp.int32, (rows, rows), 0) < lax.broadcasted_iota(
@@ -224,7 +250,6 @@
                 mix[0, here[0], here[1]] = tops.astype(jnp.bfloat16)
                 mix[1, here[0], here[1]] = rest.astype(jnp.bfloat16)
 
-    ff = win_ref.shape[2]
     count = ff // PIECES
     pieces = []
     for piece in range(PIECES):
@@ -232,10 +257,9 @@
         for side in (0, 1):
             there = pl.ds((2 * side + member) * ff + piece * count, count)
             pieces.append((win_ref.at[0, side, here], win2.at[there]))
-    for piece in range(PIECES):
-        here = pl.ds(piece * count, count)
-        there = pl.ds(member * ff + piece * count, count)
-        pieces.append((wout_ref.at[0, here], wout2.at[there]))
+    for chunk in range(CHUNKS):
+        there = wout2[chunk].at[mine_out]
+        pieces.append((there, there))
     weights, kept = [], []
 
     def weight_go(src, dst):
@@ -250,9 +274,12 @@
                 device_id_type=MESH,
             )
         )
+        if k < 2 * PIECES:
+            kept.append(pltpu.make_async_copy(src, dst, wl_sem.at[k]))
+            kept[-1].start()
+        else:
+            own_out[k - 2 * PIECES].wait()
         weights[-1].start()
-        kept.append(pltpu.make_async_copy(src, dst, wl_sem.at[k]))
-        kept[-1].start()
 
     def forward(copies):
         relays, forwards, _ = copies
@@ -263,31 +290,31 @@
     exchanges = []
     for chunk in range(CHUNKS):
         while queue and 2 * queue[0][0] + queue[0][1] <= 2 * chunk + last:
+            if queue[0] == (0, last):
+                for sent in metas:
+                    sent.wait_recv()
+                build_pick()
             z_go(*queue.pop(0))
         for _ in range(EARLY[chunk] if queue else len(pieces)):
             weight_go(*pieces.pop(0))
-        if chunk == 0:
-            for sent in metas:
-                sent.wait_recv()
-            build_pick()
-        else:
+        if chunk:
             forward(exchanges[-1])
         for way in (0, 1):
             z_sent[way, last, chunk].wait_recv()
 
         @pl.loop(0, COLS)
         def _(column):
-            send[chunk, column] = jnp.dot(
-                pick[column], held[chunk], preferred_element_type=jnp.float32
+            send[chunk][column] = jnp.dot(
+                pick[column], held[chunk][...], preferred_element_type=jnp.float32
             ).astype(jnp.bfloat16)
 
         copies = xy_copies(
-            send.at[chunk], recv.at[chunk], relay.at[chunk], xs_sem.at[chunk], xr_sem.at[chunk]
+            send[chunk], recv[chunk], relay[chunk], xs_sem.at[chunk], xr_sem.at[chunk]
         )
         for sent in copies[0] + copies[2]:
             sent.start()
         exchanges.append(copies)
-        recv[chunk, mine] = send[chunk, mine]
+        recv[chunk][mine] = send[chunk][mine]
     build_mix()
     forward(exchanges[-1])
 
@@ -305,7 +332,7 @@
         def _(step):
             here = pl.ds(pl.multiple_of(step * tile, tile), tile)
             term = lax.dot_general(
-                recv[chunk, pl.ds(step * group, group)].reshape(tile, size),
+                recv[chunk][pl.ds(step * group, group)].reshape(tile, WIDTHS[chunk]),
                 win2[:, span(chunk)],
                 (((1,), (1,)), ((), ())),
                 preferred_element_type=jnp.float32,
@@ -315,7 +342,7 @@
             if chunk < CHUNKS - 1:
                 act[here] = term
             else:
-                side = wout2.shape[0]
+                side = hidden.shape[1]
                 value = term[:, :side]
                 value = value / (1.0 + jnp.exp(-value)) * term[:, side:]
                 hidden[here] = value.astype(jnp.bfloat16)
@@ -323,29 +350,28 @@
     for relays, forwards, direct in exchanges:
         for sent in relays + forwards + direct:
             sent.wait_send()
-    for k in range(2 * PIECES, 3 * PIECES):
-        weights[k].wait_recv()
-        kept[k].wait()
 
     exchanges, r_sent = [], {}
 
     def produce(chunk):
+        weights[2 * PIECES + chunk].wait_recv()
+
         @pl.loop(0, 4)
         def _(step):
             here = pl.ds(pl.multiple_of(step * tile, tile), tile)
-            send[chunk, pl.ds(step * group, group)] = (
-                jnp.dot(hidden[here], wout2[:, span(chunk)], preferred_element_type=jnp.float32)
+            send[chunk][pl.ds(step * group, group)] = (
+                jnp.dot(hidden[here], wout2[chunk][...], preferred_element_type=jnp.float32)
                 .astype(jnp.bfloat16)
-                .reshape(group, slots, size)
+                .reshape(group, slots, WIDTHS[chunk])
             )
 
         copies = xy_copies(
-            send.at[chunk], back.at[chunk], relay2.at[chunk], bs_sem.at[chunk], br_sem.at[chunk]
+            send[chunk], back[chunk], relay2[chunk], bs_sem.at[chunk], br_sem.at[chunk]
         )
         for sent in copies[0] + copies[2]:
             sent.start()
         exchanges.append(copies)
-        back[chunk, mine] = send[chunk, mine]
+        back[chunk][mine] = send[chunk][mine]
 
     def merge(chunk):
         _, forwards, direct = exchanges[chunk]
@@ -356,8 +382,8 @@
         @pl.loop(0, RING * rows // block)
         def _(step):
             here = pl.ds(pl.multiple_of(step * block, block), block)
-            values = back[chunk].reshape(COLS * slots, size)
-            part[chunk, here] = jnp.dot(
+            values = back[chunk][...].reshape(COLS * slots, WIDTHS[chunk])
+            part[chunk][here] = jnp.dot(
                 mix[0, here], values, preferred_element_type=jnp.float32
             ) + jnp.dot(mix[1, here], values, preferred_element_type=jnp.float32)
 
@@ -367,28 +393,28 @@
             target = (m + (ahead if way == 0 else RING - ahead)) % RING
             count = half if step == 0 else rows
             first = way * half if step == 0 else 0
-            value = part[chunk, pl.ds(target * rows + first, count)]
+            value = part[chunk][pl.ds(target * rows + first, count)]
             local = pl.ds(first, count)
             if step == 0:
-                go[chunk, way, step, local] = value.astype(jnp.bfloat16)
+                go[chunk][way, step, local] = value.astype(jnp.bfloat16)
             else:
                 r_sent[way, step - 1, chunk].wait_recv()
                 if step == 1:
                     touched = pl.ds(way * half, half)
                     other = (1 - way) * half
-                    arrived = come[chunk, way, 0, touched].astype(jnp.float32)
-                    go[chunk, way, 1, touched] = (
+                    arrived = come[chunk][way, 0, touched].astype(jnp.float32)
+                    go[chunk][way, 1, touched] = (
                         value[way * half : way * half + half] + arrived
                     ).astype(jnp.bfloat16)
-                    go[chunk, way, 1, pl.ds(other, half)] = value[other : other + half].astype(
+                    go[chunk][way, 1, pl.ds(other, half)] = value[other : other + half].astype(
                         jnp.bfloat16
                     )
                 else:
-                    arrived = come[chunk, way, step - 1].astype(jnp.float32)
-                    go[chunk, way, step] = (value + arrived).astype(jnp.bfloat16)
+                    arrived = come[chunk][way, step - 1].astype(jnp.float32)
+                    go[chunk][way, step] = (value + arrived).astype(jnp.bfloat16)
             sent = pltpu.make_async_remote_copy(
-                src_ref=go.at[chunk, way, step, local],
-                dst_ref=come.at[chunk, way, step, local],
+                src_ref=go[chunk].at[way, step, local],
+                dst_ref=come[chunk].at[way, step, local],
                 send_sem=rs_sem.at[way, step, chunk],
                 recv_sem=rr_sem.at[way, step, chunk],
                 device_id={"ep": ends[way]},
@@ -399,15 +425,15 @@
             r_sent[way, step, chunk] = sent
 
     def finish(chunk):
-        total = part[chunk, pl.ds(m * rows, rows)]
+        total = part[chunk][pl.ds(m * rows, rows)]
         for way in (0, 1):
             r_sent[way, last, chunk].wait_recv()
-            total += come[chunk, way, last].astype(jnp.float32)
+            total += come[chunk][way, last].astype(jnp.float32)
         out_ref[:, span(chunk)] = total.astype(jnp.bfloat16)
 
     produce(0)
+    forward(exchanges[0])
     produce(1)
-    forward(exchanges[0])
     for chunk in range(CHUNKS):
         merge(chunk)
         reduce_step(chunk, 0)
@@ -435,44 +461,51 @@
     _, two, ff, _ = w_in.shape
     slots = RING * CAPE
     steps = RING // 2
-    size = width // CHUNKS
     kind = tokens.dtype
     dma = pltpu.SemaphoreType.DMA
+
+    def per_chunk(*lead, kind=kind):
+        return [pltpu.VMEM(lead + (size,), kind) for size in WIDTHS]
+
     return pl.pallas_call(
         layer_kernel,
         out_shape=jax.ShapeDtypeStruct((rows, width), kind),
-        in_specs=[pl.BlockSpec(memory_space=pl.ANY)]
-        + [pl.BlockSpec(memory_space=pltpu.VMEM)] * 3
+        in_specs=[pl.BlockSpec(memory_space=pl.ANY)] * 3
+        + [pl.BlockSpec(memory_space=pltpu.VMEM)]
         + [pl.BlockSpec(memory_space=pl.ANY)] * 2,
         out_specs=pl.BlockSpec(memory_space=pltpu.VMEM),
         scratch_shapes=[
-            pltpu.VMEM((CHUNKS, RING * rows, size), kind),
+            per_chunk(RING * rows),
+            pltpu.VMEM(ids.shape, ids.dtype),
+            pltpu.VMEM(gates.shape, gates.dtype),
             pltpu.VMEM((Z // GROUP, 2, COLS, 2 * rows), jnp.float32),
             pltpu.VMEM((RING, 2, COLS, 2 * rows), jnp.float32),
             pltpu.VMEM((COLS, slots, RING * rows), kind),
-            pltpu.VMEM((CHUNKS, COLS, slots, size), kind),
-            pltpu.VMEM((CHUNKS, COLS, slots, size), kind),
-            pltpu.VMEM((CHUNKS, 2 * Y, slots // 2, size), kind),
+            per_chunk(COLS, slots),
+            per_chunk(COLS, slots),
+            per_chunk(2 * Y, slots // 2),
             pltpu.VMEM((two * 2 * ff, width), kind),
-            pltpu.VMEM((2 * ff, width), kind),
+            per_chunk(2 * ff),
             pltpu.VMEM((COLS * slots, two * 2 * ff), jnp.float32),
             pltpu.VMEM((COLS * slots, 2 * ff), kind),
-            pltpu.VMEM((CHUNKS, COLS, slots, size), kind),
-            pltpu.VMEM((CHUNKS, 2 * Y, slots // 2, size), kind),
+            per_chunk(COLS, slots),
+            per_chunk(2 * Y, slots // 2),
             pltpu.VMEM((2, RING * rows, COLS * slots), kind),
-            pltpu.VMEM((CHUNKS, RING * rows, size), jnp.float32),
-            pltpu.VMEM((CHUNKS, 2, steps, rows, size), kind),
-            pltpu.VMEM((CHUNKS, 2, steps, rows, size), kind),
+            per_chunk(RING * rows, kind=jnp.float32),
+            per_chunk(2, steps, rows),
+            per_chunk(2, steps, rows),
             dma((CHUNKS,)),
+            dma((2,)),
             dma((2, steps, CHUNKS)),
             dma((2, steps, CHUNKS)),
             dma((RING - 1,)),
             dma((RING - 1,)),
             dma((CHUNKS, XY_COPIES)),
             dma((CHUNKS, XY_COPIES)),
-            dma((3 * PIECES,)),
-            dma((3 * PIECES,)),
-            dma((3 * PIECES,)),
+            dma((2 * PIECES + CHUNKS,)),
+            dma((2 * PIECES + CHUNKS,)),
+            dma((2 * PIECES,)),
+            dma((CHUNKS,)),
             dma((2, steps, CHUNKS)),
             dma((2, steps, CHUNKS)),
             dma((CHUNKS, XY_COPIES)),
@@ -486,7 +519,7 @@
 
 
 def local(tokens, gates, expert_ids, slot_expert, w_in, w_out):
-    expert = slot_expert.reshape(COLS, Z // GROUP).T.reshape(-1, 1)
+    expert = slot_expert.reshape(1, -1)
     return layer(tokens, expert_ids.T, gates.T, expert, w_in, w_out)
 
 

time: 216 us -> 203 us (0.940)
  the two profiles are of different devices: /device:TPU:60 before, /device:TPU:44 now
where the time goes in v5:
time: 203 us
  Pallas kernels  202 us (100%)
    pallas_call x1, Pallas kernels, layer(): pl.pallas_call(layer_kernel, out_shape=jax.ShapeDtypeStruct((rows, width)...  202 us

profile of v5, /device:TPU:44, one launch (start us, length us, event | category | flops | bytes accessed | tf_op | source)
XLA Modules:
  0.0 203.3 jit_solution(3981004596750200367)
XLA Ops:
  0.0 201.6 %layer.1 = bf16[64,2048]{1,0:T(8,128)(2,1)} custom-call(bf16[64,2048]{1,0:T(8,128)(2,1)} %tok_ref.1, s32[8,64]{1,0:T(8,128)} %bitcast.3, f32[8,64]{1,0:T(8,128)} %bitcast.4, s32[1,32]{1,0:T(1,128)} %bitcast.5, bf16[1,2,192,2048]{3,2,1,0:T(8,128)(2,1)} %win_ref.1, bf16[1,192,2048]{2,1,0:T(8,128)(2,1)} %wout_ref.1), custom_call_target="tpu_custom_call" | custom-call | tf_op jit(solution)/shard_map/layer/pallas_call | solution.py:470
  201.7 1.7 copy.8

commit v6 on v5

--- a/solution.py
+++ b/solution.py
@@ -16,6 +16,7 @@
 WIDTHS = (512, 512, 512, 512)
 CHUNKS = len(WIDTHS)
 PIECES = 4
+SKEW = 1.5
 EARLY = (0, 2, 2, 2)
 
 
@@ -147,28 +148,29 @@
     def z_go(chunk, step):
         if step == 0:
             own[chunk].wait()
-        for way in (0, 1):
-            if step:
-                z_sent[way, step - 1, chunk].wait_recv()
-            owner = (m + (RING - step if way == 0 else step)) % RING
-            count = half if step == last else rows
-            first = way * half if step == last else 0
-            there = held[chunk].at[pl.ds(owner * rows + first, count)]
-            sent = pltpu.make_async_remote_copy(
-                src_ref=there,
-                dst_ref=there,
-                send_sem=zs_sem.at[way, step, chunk],
-                recv_sem=zr_sem.at[way, step, chunk],
-                device_id={"ep": ends[way]},
-                device_id_type=MESH,
-            )
-            sent.start()
-            z_sent[way, step, chunk] = sent
-            started.append(sent)
+        for part_of in (0, 1):
+            for way in (0, 1):
+                if step == last and way != part_of:
+                    continue
+                if step:
+                    z_sent[way, step - 1, chunk, part_of].wait_recv()
+                owner = (m + (RING - step if way == 0 else step)) % RING
+                there = held[chunk].at[pl.ds(owner * rows + part_of * half, half)]
+                sent = pltpu.make_async_remote_copy(
+                    src_ref=there,
+                    dst_ref=there,
+                    send_sem=zs_sem.at[way, step, chunk, part_of],
+                    recv_sem=zr_sem.at[way, step, chunk, part_of],
+                    device_id={"ep": ends[way]},
+                    device_id_type=MESH,
+                )
+                sent.start()
+                z_sent[way, step, chunk, part_of] = sent
+                started.append(sent)
 
     queue = sorted(
         ((chunk, step) for chunk in range(CHUNKS) for step in range(last + 1)),
-        key=lambda place: (2 * place[0] + place[1], place[0]),
+        key=lambda place: (SKEW * place[0] + place[1], place[0]),
     )
     z_go(*queue.pop(0))
 
@@ -289,7 +291,7 @@
 
     exchanges = []
     for chunk in range(CHUNKS):
-        while queue and 2 * queue[0][0] + queue[0][1] <= 2 * chunk + last:
+        while queue and SKEW * queue[0][0] + queue[0][1] <= SKEW * chunk + last:
             if queue[0] == (0, last):
                 for sent in metas:
                     sent.wait_recv()
@@ -300,7 +302,8 @@
         if chunk:
             forward(exchanges[-1])
         for way in (0, 1):
-            z_sent[way, last, chunk].wait_recv()
+            z_sent[way, last - 1, chunk, 1 - way].wait_recv()
+            z_sent[way, last, chunk, way].wait_recv()
 
         @pl.loop(0, COLS)
         def _(column):
@@ -388,46 +391,36 @@
             ) + jnp.dot(mix[1, here], values, preferred_element_type=jnp.float32)
 
     def reduce_step(chunk, step):
-        for way in (0, 1):
-            ahead = RING // 2 - step
-            target = (m + (ahead if way == 0 else RING - ahead)) % RING
-            count = half if step == 0 else rows
-            first = way * half if step == 0 else 0
-            value = part[chunk][pl.ds(target * rows + first, count)]
-            local = pl.ds(first, count)
-            if step == 0:
+        for part_of in (0, 1):
+            local = pl.ds(part_of * half, half)
+            for way in (0, 1):
+                if step == 0 and way != part_of:
+                    continue
+                ahead = RING // 2 - step
+                target = (m + (ahead if way == 0 else RING - ahead)) % RING
+                value = part[chunk][pl.ds(target * rows + part_of * half, half)]
+                before = r_sent.get((way, step - 1, chunk, part_of))
+                if before is not None:
+                    before.wait_recv()
+                    value += come[chunk][way, step - 1, local].astype(jnp.float32)
                 go[chunk][way, step, local] = value.astype(jnp.bfloat16)
-            else:
-                r_sent[way, step - 1, chunk].wait_recv()
-                if step == 1:
-                    touched = pl.ds(way * half, half)
-                    other = (1 - way) * half
-                    arrived = come[chunk][way, 0, touched].astype(jnp.float32)
-                    go[chunk][way, 1, touched] = (
-                        value[way * half : way * half + half] + arrived
-                    ).astype(jnp.bfloat16)
-                    go[chunk][way, 1, pl.ds(other, half)] = value[other : other + half].astype(
-                        jnp.bfloat16
-                    )
-                else:
-                    arrived = come[chunk][way, step - 1].astype(jnp.float32)
-                    go[chunk][way, step] = (value + arrived).astype(jnp.bfloat16)
-            sent = pltpu.make_async_remote_copy(
-                src_ref=go[chunk].at[way, step, local],
-                dst_ref=come[chunk].at[way, step, local],
-                send_sem=rs_sem.at[way, step, chunk],
-                recv_sem=rr_sem.at[way, step, chunk],
-                device_id={"ep": ends[way]},
-                device_id_type=MESH,
-            )
-            sent.start()
-            started.append(sent)
-            r_sent[way, step, chunk] = sent
+                sent = pltpu.make_async_remote_copy(
+                    src_ref=go[chunk].at[way, step, local],
+                    dst_ref=come[chunk].at[way, step, local],
+                    send_sem=rs_sem.at[way, step, chunk, part_of],
+                    recv_sem=rr_sem.at[way, step, chunk, part_of],
+                    device_id={"ep": ends[way]},
+                    device_id_type=MESH,
+                )
+                sent.start()
+                started.append(sent)
+                r_sent[way, step, chunk, part_of] = sent
 
     def finish(chunk):
         total = part[chunk][pl.ds(m * rows, rows)]
         for way in (0, 1):
-            r_sent[way, last, chunk].wait_recv()
+            for part_of in (0, 1):
+                r_sent[way, last, chunk, part_of].wait_recv()
             total += come[chunk][way, last].astype(jnp.float32)
         out_ref[:, span(chunk)] = total.astype(jnp.bfloat16)
 
@@ -437,16 +430,19 @@
     for chunk in range(CHUNKS):
         merge(chunk)
         reduce_step(chunk, 0)
+        if chunk:
+            reduce_step(chunk - 1, 2)
         if chunk + 1 < CHUNKS:
             forward(exchanges[chunk + 1])
         if chunk + 2 < CHUNKS:
             produce(chunk + 2)
+        reduce_step(chunk, 1)
         if chunk:
             reduce_step(chunk - 1, 3)
-        reduce_step(chunk, 1)
-        if chunk:
-            finish(chunk - 1)
-        reduce_step(chunk, 2)
+        if chunk > 1:
+            finish(chunk - 2)
+    reduce_step(CHUNKS - 1, 2)
+    finish(CHUNKS - 2)
     reduce_step(CHUNKS - 1, 3)
     finish(CHUNKS - 1)
     for relays, forwards, direct in exchanges:
@@ -496,8 +492,8 @@
             per_chunk(2, steps, rows),
             dma((CHUNKS,)),
             dma((2,)),
-            dma((2, steps, CHUNKS)),
-            dma((2, steps, CHUNKS)),
+            dma((2, steps, CHUNKS, 2)),
+            dma((2, steps, CHUNKS, 2)),
             dma((RING - 1,)),
             dma((RING - 1,)),
             dma((CHUNKS, XY_COPIES)),
@@ -506,8 +502,8 @@
             dma((2 * PIECES + CHUNKS,)),
             dma((2 * PIECES,)),
             dma((CHUNKS,)),
-            dma((2, steps, CHUNKS)),
-            dma((2, steps, CHUNKS)),
+            dma((2, steps, CHUNKS, 2)),
+            dma((2, steps, CHUNKS, 2)),
             dma((CHUNKS, XY_COPIES)),
             dma((CHUNKS, XY_COPIES)),
         ],

time: 203 us -> 195 us (0.961)
  the two profiles are of different devices: /device:TPU:44 before, /device:TPU:32 now
where the time goes in v6:
time: 195 us
  Pallas kernels  193 us (99%)
    pallas_call x1, Pallas kernels, layer(): pl.pallas_call(layer_kernel, out_shape=jax.ShapeDtypeStruct((rows, width)...  193 us

profile of v6, /device:TPU:32, one launch (start us, length us, event | category | flops | bytes accessed | tf_op | source)
XLA Modules:
  0.0 194.8 jit_solution(795821067415219637)
XLA Ops:
  0.0 193.1 %layer.1 = bf16[64,2048]{1,0:T(8,128)(2,1)} custom-call(bf16[64,2048]{1,0:T(8,128)(2,1)} %tok_ref.1, s32[8,64]{1,0:T(8,128)} %bitcast.3, f32[8,64]{1,0:T(8,128)} %bitcast.4, s32[1,32]{1,0:T(1,128)} %bitcast.5, bf16[1,2,192,2048]{3,2,1,0:T(8,128)(2,1)} %win_ref.1, bf16[1,192,2048]{2,1,0:T(8,128)(2,1)} %wout_ref.1), custom_call_target="tpu_custom_call" | custom-call | tf_op jit(solution)/shard_map/layer/pallas_call | solution.py:466
  193.1 1.7 copy.8

commit v7 on v6

--- a/solution.py
+++ b/solution.py
@@ -16,8 +16,8 @@
 WIDTHS = (512, 512, 512, 512)
 CHUNKS = len(WIDTHS)
 PIECES = 4
-SKEW = 1.5
-EARLY = (0, 2, 2, 2)
+SKEW = 1
+EARLY = (1, 1, 2, 2)
 
 
 def z_place():

time: 195 us -> 195 us (level)
  the two profiles are of different devices: /device:TPU:32 before, /device:TPU:16 now
where the time goes in v7:
time: 195 us
  Pallas kernels  193 us (99%)
    pallas_call x1, Pallas kernels, layer(): pl.pallas_call(layer_kernel, out_shape=jax.ShapeDtypeStruct((rows, width)...  193 us

profile of v7, /device:TPU:16, one launch (start us, length us, event | category | flops | bytes accessed | tf_op | source)
XLA Modules:
  0.0 194.8 jit_solution(12548740191277149016)
XLA Ops:
  0.0 193.1 %layer.1 = bf16[64,2048]{1,0:T(8,128)(2,1)} custom-call(bf16[64,2048]{1,0:T(8,128)(2,1)} %tok_ref.1, s32[8,64]{1,0:T(8,128)} %bitcast.3, f32[8,64]{1,0:T(8,128)} %bitcast.4, s32[1,32]{1,0:T(1,128)} %bitcast.5, bf16[1,2,192,2048]{3,2,1,0:T(8,128)(2,1)} %win_ref.1, bf16[1,192,2048]{2,1,0:T(8,128)(2,1)} %wout_ref.1), custom_call_target="tpu_custom_call" | custom-call | tf_op jit(solution)/shard_map/layer/pallas_call | solution.py:466
  193.1 1.7 copy.8

commit v8 on v7

--- a/solution.py
+++ b/solution.py
@@ -17,7 +17,7 @@
 CHUNKS = len(WIDTHS)
 PIECES = 4
 SKEW = 1
-EARLY = (1, 1, 2, 2)
+EARLY = (0, 2, 2, 2)
 
 
 def z_place():

time: 195 us -> 192 us (0.985)
  the two profiles are of different devices: /device:TPU:16 before, /device:TPU:4 now
where the time goes in v8:
time: 192 us
  Pallas kernels  191 us (99%)
    pallas_call x1, Pallas kernels, layer(): pl.pallas_call(layer_kernel, out_shape=jax.ShapeDtypeStruct((rows, width)...  191 us

profile of v8, /device:TPU:4, one launch (start us, length us, event | category | flops | bytes accessed | tf_op | source)
XLA Modules:
  0.0 192.3 jit_solution(7553585068335289694)
XLA Ops:
  0.0 190.6 %layer.1 = bf16[64,2048]{1,0:T(8,128)(2,1)} custom-call(bf16[64,2048]{1,0:T(8,128)(2,1)} %tok_ref.1, s32[8,64]{1,0:T(8,128)} %bitcast.3, f32[8,64]{1,0:T(8,128)} %bitcast.4, s32[1,32]{1,0:T(1,128)} %bitcast.5, bf16[1,2,192,2048]{3,2,1,0:T(8,128)(2,1)} %win_ref.1, bf16[1,192,2048]{2,1,0:T(8,128)(2,1)} %wout_ref.1), custom_call_target="tpu_custom_call" | custom-call | tf_op jit(solution)/shard_map/layer/pallas_call | solution.py:466
  190.7 1.7 copy.8
